TPU v7x, 32 devices: a whole 2x2x4 slice. The times are simulated.
32 devices in a mesh: ctx: 8 (over z, x), tp: 4 (over y, core).
Axes of the slice: x: 2, y: 2, z: 4, core: 2. Of those that a mesh axis runs over, the one named last changes fastest.
Arguments:
- hidden: bfloat16 [1024, 3584], P('ctx', 'tp'), may hold values from -6 to 6
- norm_gain: float32 [3584], replicated, may hold values from 0.1 to 1.9
- w_query: bfloat16 [3584, 3584], P(None, 'tp'), may hold values from -0.09375 to 0.09375
- bias_query: float32 [3584], P('tp'), may hold values from -3 to 3
- w_key: bfloat16 [3584, 512], P(None, 'tp'), may hold values from -0.09375 to 0.09375
- bias_key: float32 [512], P('tp'), may hold values from -3 to 3
- w_value: bfloat16 [3584, 512], P(None, 'tp'), may hold values from -0.09375 to 0.09375
- bias_value: float32 [512], P('tp'), may hold values from -3 to 3
- cache_key: bfloat16 [2048, 512], P('ctx', 'tp'), may hold values from -64 to 64
- cache_value: bfloat16 [2048, 512], P('ctx', 'tp'), may hold values from -6 to 6
- keep: int32 [1024], replicated, may hold values from 0 to 1, as said below
- positions: int32 [3, 1024], replicated, may hold values from 0 to 2047
Outputs:
- attended: bfloat16 [1024, 3584], P('ctx', 'tp')
Inputs may be any that keep to these rules, and one draw needn't show every extreme that they name: `keep`: exactly 512 tokens are kept; the counts kept by the 128-token blocks differ widely, and some block keeps all of its tokens.
All inputs are finite; a program needn't handle non-finite values.
Results may differ from a plain program's by a relative error of at most 0.0075.
The roundings to bfloat16 on the way count: a program that leaves them out, or rounds other values in their place, can miss the bound.
Values may be sent and summed in bfloat16 or wider, within the bound.
No kernel may reach another device: no remote copies, remote signals or barrier semaphores. Data moves between devices by JAX's collectives and lax.ppermute only.
A program may use at most 128 MiB of HBM per device.

v0:
```python
import functools

import jax
import jax.numpy as jnp
from jax import lax
from jax.experimental import pallas as pl
from jax.experimental.pallas import tpu as pltpu
from jax.sharding import PartitionSpec as P


HD = 128
LOG2E = 1.4426950408889634

EARLY = 4


def swap(x, axis, n, k):
    return lax.ppermute(x, axis, [(i, i ^ k) for i in range(n)])


def flip(row):
    n = row.shape[1]
    eye = lax.broadcasted_iota(jnp.int32, (n, n), 0) == lax.broadcasted_iota(jnp.int32, (n, n), 1)
    return jnp.sum(jnp.where(eye, row, jnp.zeros_like(row)), axis=1, keepdims=True)


def start_copies(pairs, sems):
    copies = [pltpu.make_async_copy(a, b, sems.at[i]) for i, (a, b) in enumerate(pairs)]
    for copy in copies:
        copy.start()
    return copies


def stack_kernel(key_in, value_in, stacked, sems):
    for copy in start_copies([(key_in, stacked.at[0]), (value_in, stacked.at[1])], sems):
        copy.wait()


def part_of(weight, me, j, parts):
    depth = weight.shape[0] // parts
    return weight.at[pl.ds(pl.multiple_of((me ^ j) * depth, depth), depth), :]


def setup_kernel(moved, parts, rank_ref, me_ref, keep_in, spots_in, w_query, *refs):
    sources, targets = refs[:moved], refs[moved : 2 * moved]
    weights, refs = refs[2 * moved : 2 * moved + EARLY], refs[2 * moved + EARLY :]
    cosine, sine, tags, order, live, keep, spots, sems = refs
    rank = rank_ref[0]
    copies = start_copies(
        [(keep_in, keep), (spots_in, spots)]
        + list(zip(sources, targets))
        + [(part_of(w_query, me_ref[0], j, parts), weight) for j, weight in enumerate(weights)],
        sems,
    )
    copies[0].wait()
    copies[1].wait()
    blocks, rows = keep.shape
    kept = keep[...].astype(jnp.float32)
    upper = lax.broadcasted_iota(jnp.int32, (rows, rows), 0) < lax.broadcasted_iota(jnp.int32, (rows, rows), 1)
    inner = jnp.dot(kept.astype(jnp.bfloat16), upper.astype(jnp.bfloat16), preferred_element_type=jnp.float32)
    counts = jnp.broadcast_to(jnp.sum(kept, axis=1, keepdims=True), (blocks, rows))
    lower = lax.broadcasted_iota(jnp.int32, (blocks, blocks), 1) < lax.broadcasted_iota(jnp.int32, (blocks, blocks), 0)
    before = jnp.dot(lower.astype(jnp.bfloat16), counts.astype(jnp.bfloat16), preferred_element_type=jnp.float32)
    ordinals = inner + before
    tags[...] = jnp.where(kept > 0, ordinals, jnp.float32(2**30))
    mine = lax.broadcasted_iota(jnp.int32, (blocks, rows), 0) == rank
    order[...] = flip(jnp.sum(jnp.where(mine, ordinals, 0.0), axis=0, keepdims=True))
    live[...] = flip(jnp.sum(jnp.where(mine, kept, 0.0), axis=0, keepdims=True))

    where = spots[:, pl.ds(pl.multiple_of(rank * rows, rows), rows)].astype(jnp.float32)
    half = HD // 2
    freq = lax.rem(lax.broadcasted_iota(jnp.int32, (1, HD), 1), half)
    inv = jnp.exp(-(2.0 * freq.astype(jnp.float32) / HD) * jnp.log(jnp.full((1, 1), 1000000.0, jnp.float32)))
    picked = jnp.where(
        freq < HD // 8,
        flip(where[0:1]),
        jnp.where(freq < HD // 8 + 3 * HD // 16, flip(where[1:2]), flip(where[2:3])),
    )
    angle = picked * inv
    cosine[...] = jnp.cos(angle)
    low = lax.broadcasted_iota(jnp.int32, (1, HD), 1) < half
    sine[...] = jnp.where(low, -1.0, 1.0) * jnp.sin(angle)
    for copy in copies[2:]:
        copy.wait()


def turn(x, cosine, sine):
    return x * cosine + pltpu.roll(x, HD // 2, 1) * sine


def wide(ref, start, count):
    block = ref[pl.ds(start, count), :]
    return jnp.concatenate([block[i : i + 1] for i in range(count)], axis=1)


def key_value_kernel(parts, *refs):
    me_ref = refs[0]
    hidden_refs = refs[1 : 1 + parts]
    gain, w_key, bias_key, w_value, bias_value, cosine, sine, normed, fresh = refs[1 + parts :]
    width = hidden_refs[0].shape[1]
    me = me_ref[0]
    square = None
    for ref in hidden_refs:
        x = ref[...].astype(jnp.float32)
        part = jnp.sum(x * x, axis=1, keepdims=True)
        square = part if square is None else square + part
    scale = lax.rsqrt(square * (1.0 / (width * parts)) + 1e-06)
    key_sum = value_sum = None
    for j, ref in enumerate(hidden_refs):
        spot = pl.multiple_of((me ^ j) * width, width)
        x = ref[...].astype(jnp.float32)
        piece = (x * scale * wide(gain, (me ^ j) * (width // HD), width // HD)).astype(jnp.bfloat16)
        normed[:, j * width : (j + 1) * width] = piece
        k = jnp.dot(piece, w_key[pl.ds(spot, width), :], preferred_element_type=jnp.float32)
        v = jnp.dot(piece, w_value[pl.ds(spot, width), :], preferred_element_type=jnp.float32)
        key_sum = k if key_sum is None else key_sum + k
        value_sum = v if value_sum is None else value_sum + v
    for h in range(key_sum.shape[1] // HD):
        cut = slice(h * HD, (h + 1) * HD)
        fresh[0, :, cut] = turn(key_sum[:, cut] + bias_key[h : h + 1, :], cosine[...], sine[...]).astype(jnp.bfloat16)
        fresh[1, :, cut] = (value_sum[:, cut] + bias_value[h : h + 1, :]).astype(jnp.bfloat16)


def query_kernel(parts, me_ref, normed, bias_query, cosine, sine, w_query, *refs):
    early, query = refs[:EARLY], refs[EARLY]
    width = normed.shape[1] // parts
    late = range(EARLY, parts)
    if late:
        weights, sems = refs[EARLY + 1 :]
        copies = start_copies([(part_of(w_query, me_ref[0], j, parts), weights.at[j - EARLY]) for j in late], sems)
    total = None
    for j in range(parts):
        if j >= EARLY:
            copies[j - EARLY].wait()
        weight = early[j][...] if j < EARLY else weights[j - EARLY]
        q = jnp.dot(normed[:, j * width : (j + 1) * width], weight, preferred_element_type=jnp.float32)
        total = q if total is None else total + q
    rows = normed.shape[0]
    for h in range(total.shape[1] // HD):
        cut = slice(h * HD, (h + 1) * HD)
        query[h * rows : (h + 1) * rows, :] = turn(
            total[:, cut] + bias_query[h : h + 1, :], cosine[...], sine[...]
        ).astype(jnp.bfloat16)


SCALE = LOG2E / (HD**0.5)


def fold(x):
    out = x[:, :HD]
    for spot in range(HD, x.shape[1], HD):
        out = out + x[:, spot : spot + HD]
    return out


def absorb(state, query, key, value, bias):
    rows, count = query.shape[0], key.shape[0]
    score = lax.dot_general(query, key, (((1,), (1,)), ((), ())), preferred_element_type=jnp.float32)
    if bias is not None:
        own = bias.shape[0]
        score = jnp.concatenate([score[r : r + own] + bias for r in range(0, rows, own)], axis=0)
    higher = jnp.broadcast_to(jnp.max(score, axis=1, keepdims=True), (rows, HD))
    if state is not None:
        peak, total, summed = state
        higher = jnp.maximum(peak, higher)
    weights = jnp.exp2((score - jnp.concatenate([higher] * (count // HD), axis=1)) * SCALE)
    sums = fold(weights)
    added = jnp.dot(weights.astype(jnp.bfloat16), value, preferred_element_type=jnp.float32)
    if state is None:
        return higher, sums, added
    shrink = jnp.exp2((peak - higher) * SCALE)
    return higher, total * shrink + sums, summed * shrink + added


def groups(segments):
    group, count = [], 0
    for segment in segments:
        group.append(segment)
        count += segment[2]
        if count >= CHUNK or segment is segments[-1]:
            yield group
            group, count = [], 0


def attend_kernel(segments, given, last, *refs):
    refs = list(refs)
    rank, query, tags, order, live = refs[0][0], *refs[1:5]
    del refs[:5]
    state = None
    if given:
        state = tuple(ref[...] for ref in refs[:3])
        del refs[:3]
    q = query[...]
    for fresh in (False, True):
        for group in groups([s for s in segments if (s[3] is not None) == fresh]):
            key, value = [
                jnp.concatenate([refs[i][kind, start : start + count] for i, start, count, unused in group], axis=0)
                for kind in range(2)
            ]
            bias = None
            if fresh:
                tag = jnp.concatenate([tags[pl.ds(rank ^ s[3], 1), :] for s in group], axis=1)
                bias = jnp.where(tag <= order[...], 0.0, -jnp.inf)
            state = absorb(state, q, key, value, bias)
    finish(refs[len({s[0] for s in segments}) :], state, live, last)


def join_kernel(cuts, *refs):
    spot = 0
    for ref, (start, count) in zip(refs, cuts):
        refs[-1][:, spot : spot + count] = ref[:, start : start + count]
        spot += count


def finish(refs, state, live, last):
    if not last:
        for ref, part in zip(refs, state):
            ref[...] = part
        return
    out = refs[0]
    count = out.shape[0]
    result = state[2] * (1.0 / jnp.sum(state[1], axis=1, keepdims=True))
    for h in range(result.shape[0] // count):
        out[:, h * HD : (h + 1) * HD] = (result[h * count : (h + 1) * count] * live[...]).astype(jnp.bfloat16)


def stacked_kernel(query, tags, order, live, cached, news, out):
    rows = query.shape[0]
    q = query[...]

    def plain(i, state):
        return absorb(state, q, cached[i, 0], cached[i, 1], None)

    def masked(i, state):
        bias = jnp.where(tags[pl.ds(i, 1), :] <= order[...], 0.0, -jnp.inf)
        return absorb(state, q, news[i, 0], news[i, 1], bias)

    state = (
        jnp.full((rows, HD), -1e30, jnp.float32),
        jnp.zeros((rows, HD), jnp.float32),
        jnp.zeros((rows, HD), jnp.float32),
    )
    state = lax.fori_loop(0, cached.shape[0], plain, state)
    state = lax.fori_loop(0, news.shape[0], masked, state)
    finish([out], state, live, True)


CHUNK = 512


def call(kernel, outs, args, scalars=0, far=(), scratch=(), flops=0, moved=0):
    many = isinstance(outs, (list, tuple))
    specs = [pl.BlockSpec(memory_space=pltpu.SMEM)] * scalars
    specs += [
        pl.BlockSpec(memory_space=pltpu.HBM if i in far else pltpu.VMEM) for i in range(scalars, len(args))
    ]
    out_specs = jax.tree.map(lambda _: pl.BlockSpec(memory_space=pltpu.VMEM), list(outs) if many else outs)
    args = [pltpu.with_memory_space_constraint(a, pltpu.HBM) if i in far else a for i, a in enumerate(args)]
    return pl.pallas_call(
        kernel,
        out_shape=list(outs) if many else outs,
        in_specs=specs,
        out_specs=out_specs,
        scratch_shapes=list(scratch),
        compiler_params=pltpu.CompilerParams(vmem_limit_bytes=20 * 1024 * 1024),
        cost_estimate=pl.CostEstimate(flops=flops, bytes_accessed=moved, transcendentals=0),
    )(*args)


def local(
    hidden,
    norm_gain,
    w_query,
    bias_query,
    w_key,
    bias_key,
    w_value,
    bias_value,
    cache_key,
    cache_value,
    keep,
    positions,
):
    n_ctx, n_tp = lax.axis_size("ctx"), lax.axis_size("tp")
    rank = lax.axis_index("ctx")[None].astype(jnp.int32)
    me = lax.axis_index("tp")[None].astype(jnp.int32)
    rows, width = hidden.shape
    kv_width = w_key.shape[1]
    heads = w_query.shape[1] // HD
    sds = jax.ShapeDtypeStruct
    f32, bf16 = jnp.float32, jnp.bfloat16

    far_hidden = swap(hidden, "tp", n_tp, 2)
    pieces = [hidden, swap(hidden, "tp", n_tp, 1), far_hidden, swap(far_hidden, "tp", n_tp, 1)]

    carried = (
        hidden,
        norm_gain.reshape(-1, HD),
        w_key,
        bias_key.reshape(-1, HD),
        w_value,
        bias_value.reshape(-1, HD),
        bias_query.reshape(-1, HD),
    )
    cache = call(
        stack_kernel,
        sds((2, *cache_key.shape), bf16),
        (cache_key, cache_value),
        far=(0, 1),
        scratch=[pltpu.SemaphoreType.DMA((2,))],
        moved=1000000,
    )
    setup = call(
        functools.partial(setup_kernel, len(carried), n_tp),
        [sds(a.shape, a.dtype) for a in carried]
        + [sds((width, heads * HD), bf16)] * EARLY
        + [
            sds((rows, HD), f32),
            sds((rows, HD), f32),
            sds((n_ctx, rows), f32),
            sds((rows, 1), f32),
            sds((rows, 1), f32),
        ],
        (rank, me, keep.reshape(n_ctx, rows), positions, w_query, *carried),
        2,
        range(2, 5 + len(carried)),
        [
            pltpu.VMEM((n_ctx, rows), jnp.int32),
            pltpu.VMEM(positions.shape, jnp.int32),
            pltpu.SemaphoreType.DMA((2 + EARLY + len(carried),)),
        ],
        0,
        4000000,
    )
    pieces[0], gain, key_weight, key_bias, value_weight, value_bias, query_bias = setup[:7]
    early = setup[7 : 7 + EARLY]
    cosine, sine, tags, own_order, live = setup[7 + EARLY :]

    normed, fresh = call(
        functools.partial(key_value_kernel, n_tp),
        (sds((rows, width * n_tp), bf16), sds((2, rows, kv_width), bf16)),
        (me, *pieces, gain, key_weight, key_bias, value_weight, value_bias, cosine, sine),
        1,
        flops=2 * rows * width * n_tp * 2 * kv_width,
        moved=3000000,
    )
    late = ()
    if n_tp > EARLY:
        late = (pltpu.VMEM((n_tp - EARLY, width, heads * HD), bf16), pltpu.SemaphoreType.DMA((n_tp - EARLY,)))
    query = call(
        functools.partial(query_kernel, n_tp),
        sds((rows * heads, HD), bf16),
        (me, normed, query_bias, cosine, sine, w_query, *early),
        1,
        (5,),
        late,
        flops=2 * rows * width * n_tp * heads * HD,
        moved=7000000,
    )
    final = sds((rows, heads * HD), bf16)
    if not paired(n_ctx):
        cached = lax.all_gather(cache, "ctx", axis=0)
        news = lax.all_gather(fresh, "ctx", axis=0)
        return call(stacked_kernel, final, (query, tags, own_order, live, cached, news))

    def attend(segments, state=None, last=False):
        arrays = []
        for array, *unused in segments:
            if not any(array is a for a in arrays):
                arrays.append(array)
        place = lambda array: [array is a for a in arrays].index(True)
        cuts = tuple((place(a), start, count, source) for a, start, count, source in segments)
        keys = sum(s[2] for s in segments)
        return call(
            functools.partial(attend_kernel, cuts, state is not None, last),
            final if last else [sds((rows * heads, HD), f32)] * 3,
            (rank, query, tags, own_order, live, *(state or ()), *arrays),
            1,
            flops=4 * rows * heads * HD * keys,
            moved=8 * rows * heads * keys,
        )

    def join(*cuts):
        out = sds((2, sum(c[2] for c in cuts), HD), bf16)
        return call(functools.partial(join_kernel, [c[1:] for c in cuts]), out, [c[0] for c in cuts])

    ctx = lambda x, k: swap(x, "ctx", n_ctx, k)
    old, new = cache.shape[1], rows
    c4 = ctx(cache, 4)
    c2 = ctx(cache, 2)
    c1 = ctx(cache, 1)
    c3 = ctx(c2, 1)
    c6 = ctx(c4, 2)
    f4 = ctx(fresh, 4)
    f2 = ctx(fresh, 2)
    f6 = ctx(f4, 2)
    ux = ctx(join((fresh, 0, new), (c4, 0, old)), 1)
    xa = ctx(join((f2, 0, new), (c6, 0, old)), 1)
    xb = ctx(join((f4, 0, new), (f6, 0, new)), 1)
    state = attend([(c, 0, old, None) for c in (cache, c2, c4, c1)])
    state = attend(
        [(c3, 0, old, None), (ux, new, old, None), (c6, 0, old, None)]
        + [(fresh, 0, new, 0), (ux, 0, new, 1), (f2, 0, new, 2), (f4, 0, new, 4), (f6, 0, new, 6)],
        state,
    )
    return attend([(xa, new, old, None), (xa, 0, new, 3), (xb, 0, new, 5), (xb, new, new, 7)], state, True)


def paired(n_ctx):
    return n_ctx == 8


def solution(mesh):
    in_specs = (
        P("ctx", "tp"),
        P(),
        P(None, "tp"),
        P("tp"),
        P(None, "tp"),
        P("tp"),
        P(None, "tp"),
        P("tp"),
        P("ctx", "tp"),
        P("ctx", "tp"),
        P(),
        P(),
    )

    return jax.shard_map(local, mesh=mesh, in_specs=in_specs, out_specs=P("ctx", "tp"), check_vma=False)
```

profile of v0, /device:TPU:0, one launch (start us, length us, event | category | flops | bytes accessed | tf_op | source)
XLA Modules:
  0.0 51.9 jit_solution(214389505237759822)
XLA Ops:
  0.0 3.0 %collective-permute-start.1 = (bf16[128,896]{1,0:T(8,128)(2,1)}, bf16[128,896]{1,0:T(8,128)(2,1)S(1)}, u32[]{:S(2)}, u32[]{:S(2)}) collective-permute-start(bf16[128,896]{1,0:T(8,128)(2,1)} %refs_0_.1), channel_id=1, source_target_pairs={{0,2},{1,3},{2,0},{3,1},{4,6},{5,7},{6,4},{7,5},{8,10},{9,11},{10,... | collective-permute-start | bytes 688136 | tf_op jit(solution)/shard_map/ppermute | solution.py:18
  3.0 0.0 collective-permute-start
  3.0 5.8 %collective-permute-done.1.refs_3_ = bf16[128,896]{1,0:T(8,128)(2,1)S(1)} collective-permute-done((bf16[128,896]{1,0:T(8,128)(2,1)}, bf16[128,896]{1,0:T(8,128)(2,1)S(1)}, u32[]{:S(2)}, u32[]{:S(2)}) %collective-permute-start.1) | collective-permute-done | bytes 229408 | tf_op jit(solution)/shard_map/ppermute | solution.py:18
  8.8 0.0 collective-permute-start.2
  8.8 0.9 %shard_map.121.refs_5_ = bf16[2,256,128]{2,1,0:T(8,128)(2,1)S(1)} custom-call(bf16[256,128]{1,0:T(8,128)(2,1)} %key_in.1, bf16[256,128]{1,0:T(8,128)(2,1)} %value_in.1), custom_call_target="tpu_custom_call" | custom-call | bytes 1000000 | tf_op jit(solution)/shard_map/pallas_call | solution.py:259
  9.7 2.9 %collective-permute-start.4 = (bf16[2,256,128]{2,1,0:T(8,128)(2,1)S(1)}, bf16[2,256,128]{2,1,0:T(8,128)(2,1)S(1)}, u32[]{:S(2)}, u32[]{:S(2)}) collective-permute-start(bf16[2,256,128]{2,1,0:T(8,128)(2,1)S(1)} %shard_map.121.refs_5_), channel_id=1, source_target_pairs={{0,16},{4,20},{8,24},{12,28},{16,0},{20,4},{24,8},{28,12},{1,17},{... | collective-permute-start | bytes 393224 | tf_op jit(solution)/shard_map/ppermute | solution.py:18
  12.6 7.0 %collective-permute-done.4.refs_7_.refs_1_ = bf16[2,256,128]{2,1,0:T(8,128)(2,1)S(1)} collective-permute-done((bf16[2,256,128]{2,1,0:T(8,128)(2,1)S(1)}, bf16[2,256,128]{2,1,0:T(8,128)(2,1)S(1)}, u32[]{:S(2)}, u32[]{:S(2)}) %collective-permute-start.4) | collective-permute-done | bytes 131104 | tf_op jit(solution)/shard_map/ppermute | solution.py:18
  19.6 0.7 %collective-permute-start.8 = (bf16[2,256,128]{2,1,0:T(8,128)(2,1)S(1)}, bf16[2,256,128]{2,1,0:T(8,128)(2,1)S(1)}, u32[]{:S(2)}, u32[]{:S(2)}) collective-permute-start(bf16[2,256,128]{2,1,0:T(8,128)(2,1)S(1)} %collective-permute-done.4.refs_7_.refs_1_), channel_id=1, source_target_pairs={{0,8},{4,12},{8,0},{12,4},{16,24},{20,28},{24,16},{28,20},{1,9},{5... | collective-permute-start | bytes 393224 | tf_op jit(solution)/shard_map/ppermute | solution.py:18
  20.3 1.3 %collective-permute-start.3 = (bf16[2,256,128]{2,1,0:T(8,128)(2,1)S(1)}, bf16[2,256,128]{2,1,0:T(8,128)(2,1)S(1)}, u32[]{:S(2)}, u32[]{:S(2)}) collective-permute-start(bf16[2,256,128]{2,1,0:T(8,128)(2,1)S(1)} %shard_map.121.refs_5_), channel_id=1, source_target_pairs={{0,8},{4,12},{8,0},{12,4},{16,24},{20,28},{24,16},{28,20},{1,9},{5... | collective-permute-start | bytes 393224 | tf_op jit(solution)/shard_map/ppermute | solution.py:18
  21.6 3.7 %shard_map.118 = (bf16[128,896]{1,0:T(8,128)(2,1)S(1)}, f32[28,128]{1,0:T(8,128)S(1)}, bf16[3584,128]{1,0:T(8,128)(2,1)S(1)}, f32[1,128]{1,0:T(1,128)S(1)}, bf16...) custom-call(s32[1]{0:T(128)} %bitcast.rank_ref.refs_0_, ...), custom_call_target="tpu_custom_call" | custom-call | bytes 4000000 | tf_op jit(solution)/shard_map/pallas_call | solution.py:259
  25.3 0.0 collective-permute-done.refs_2_
  25.3 0.0 collective-permute-done.2.refs_4_
  25.3 0.9 %shard_map.119 = (bf16[128,3584]{1,0:T(8,128)(2,1)S(1)}, bf16[2,128,128]{2,1,0:T(8,128)(2,1)S(1)}) custom-call(s32[1]{0:T(128)} %bitcast.1.me_ref.refs_0_, bf16[128,896]{1,0:T(8,128)(2,1)S(1)} %get-tuple-element.29.refs_1_, bf16[128,896]{1,0:T(8,128)(2,1)S(1)} %collective-permute-done.refs_2_, bf16[128,896]{1,0:T(8,128)(2,1)S(1)} %collective-permute-done.1.refs_3_, ...), custom_call_target="tpu_custom_call" | custom-call | flops 234881024 | bytes 3000000 | tf_op jit(solution)/shard_map/pallas_call | solution.py:259
  26.3 2.2 %collective-permute-start.10 = (bf16[2,128,128]{2,1,0:T(8,128)(2,1)S(1)}, bf16[2,128,128]{2,1,0:T(8,128)(2,1)S(1)}, u32[]{:S(2)}, u32[]{:S(2)}) collective-permute-start(bf16[2,128,128]{2,1,0:T(8,128)(2,1)S(1)} %get-tuple-element.49.refs_0_.refs_11_), channel_id=1, source_target_pairs={{0,16},{4,20},{8,24},{12,28},{16,0},{20,4},{24,8},{28,12},{1,17},{... | collective-permute-start | bytes 196616 | tf_op jit(solution)/shard_map/ppermute | solution.py:18
  28.4 2.0 %collective-permute-start.9 = (bf16[2,128,128]{2,1,0:T(8,128)(2,1)S(1)}, bf16[2,128,128]{2,1,0:T(8,128)(2,1)S(1)}, u32[]{:S(2)}, u32[]{:S(2)}) collective-permute-start(bf16[2,128,128]{2,1,0:T(8,128)(2,1)S(1)} %get-tuple-element.49.refs_0_.refs_11_), channel_id=1, source_target_pairs={{0,8},{4,12},{8,0},{12,4},{16,24},{20,28},{24,16},{28,20},{1,9},{5... | collective-permute-start | bytes 196616 | tf_op jit(solution)/shard_map/ppermute | solution.py:18
  30.5 1.6 %collective-permute-start.7 = (bf16[2,384,128]{2,1,0:T(8,128)(2,1)S(1)}, bf16[2,384,128]{2,1,0:T(8,128)(2,1)S(1)}, u32[]{:S(2)}, u32[]{:S(2)}) collective-permute-start(bf16[2,384,128]{2,1,0:T(8,128)(2,1)S(1)} %shard_map.123), channel_id=1, source_target_pairs={{0,4},{4,0},{8,12},{12,8},{16,20},{20,16},{24,28},{28,24},{1,5},{5... | collective-permute-start | bytes 589832 | tf_op jit(solution)/shard_map/ppermute | solution.py:18
  32.0 0.0 collective-permute-done.10.refs_13_.refs_0_
  32.0 0.9 %collective-permute-start.11 = (bf16[2,128,128]{2,1,0:T(8,128)(2,1)S(1)}, bf16[2,128,128]{2,1,0:T(8,128)(2,1)S(1)}, u32[]{:S(2)}, u32[]{:S(2)}) collective-permute-start(bf16[2,128,128]{2,1,0:T(8,128)(2,1)S(1)} %collective-permute-done.10.refs_13_.refs_0_), channel_id=1, source_target_pairs={{0,8},{4,12},{8,0},{12,4},{16,24},{20,28},{24,16},{28,20},{1,9},{5... | collective-permute-start | bytes 196616 | tf_op jit(solution)/shard_map/ppermute | solution.py:18
  32.9 0.0 collective-permute-done.8.refs_10_.refs_1_
  32.9 1.5 %collective-permute-start.5 = (bf16[2,256,128]{2,1,0:T(8,128)(2,1)S(1)}, bf16[2,256,128]{2,1,0:T(8,128)(2,1)S(1)}, u32[]{:S(2)}, u32[]{:S(2)}) collective-permute-start(bf16[2,256,128]{2,1,0:T(8,128)(2,1)S(1)} %shard_map.121.refs_5_), channel_id=1, source_target_pairs={{0,4},{4,0},{8,12},{12,8},{16,20},{20,16},{24,28},{28,24},{1,5},{5... | collective-permute-start | bytes 393224 | tf_op jit(solution)/shard_map/ppermute | solution.py:18
  34.4 0.0 collective-permute-done.9.refs_12_.refs_0_
  34.4 0.6 %collective-permute-start.12 = (bf16[2,384,128]{2,1,0:T(8,128)(2,1)S(1)}, bf16[2,384,128]{2,1,0:T(8,128)(2,1)S(1)}, u32[]{:S(2)}, u32[]{:S(2)}) collective-permute-start(bf16[2,384,128]{2,1,0:T(8,128)(2,1)S(1)} %shard_map.125), channel_id=1, source_target_pairs={{0,4},{4,0},{8,12},{12,8},{16,20},{20,16},{24,28},{28,24},{1,5},{5... | collective-permute-start | bytes 589832 | tf_op jit(solution)/shard_map/ppermute | solution.py:18
  35.0 0.0 collective-permute-done.3.refs_6_
  35.0 1.5 %collective-permute-start.6 = (bf16[2,256,128]{2,1,0:T(8,128)(2,1)S(1)}, bf16[2,256,128]{2,1,0:T(8,128)(2,1)S(1)}, u32[]{:S(2)}, u32[]{:S(2)}) collective-permute-start(bf16[2,256,128]{2,1,0:T(8,128)(2,1)S(1)} %collective-permute-done.3.refs_6_), channel_id=1, source_target_pairs={{0,4},{4,0},{8,12},{12,8},{16,20},{20,16},{24,28},{28,24},{1,5},{5... | collective-permute-start | bytes 393224 | tf_op jit(solution)/shard_map/ppermute | solution.py:18
  36.5 0.0 collective-permute-done.11.refs_14_.refs_1_
  36.5 1.2 %collective-permute-start.13 = (bf16[2,256,128]{2,1,0:T(8,128)(2,1)S(1)}, bf16[2,256,128]{2,1,0:T(8,128)(2,1)S(1)}, u32[]{:S(2)}, u32[]{:S(2)}) collective-permute-start(bf16[2,256,128]{2,1,0:T(8,128)(2,1)S(1)} %shard_map.126), channel_id=1, source_target_pairs={{0,4},{4,0},{8,12},{12,8},{16,20},{20,16},{24,28},{28,24},{1,5},{5... | collective-permute-start | bytes 393224 | tf_op jit(solution)/shard_map/ppermute | solution.py:18
  37.7 1.4 %shard_map.120.refs_1_ = bf16[896,128]{1,0:T(8,128)(2,1)S(1)} custom-call(s32[1]{0:T(128)} %bitcast.1.me_ref.refs_0_, bf16[128,3584]{1,0:T(8,128)(2,1)S(1)} %get-tuple-element.37.normed, f32[7,128]{1,0:T(8,128)S(1)} %get-tuple-element.38.bias_query, f32[128,128]{1,0:T(8,128)S(1)} %get-tuple-element.35.refs_10_.cosine, ...), custom_call_target="tpu_custom_call" | custom-call | flops 822083584 | bytes 7000000 | tf_op jit(solution)/shard_map/pallas_call | solution.py:259
  39.1 2.0 %collective-permute-done.5.refs_8_ = bf16[2,256,128]{2,1,0:T(8,128)(2,1)S(1)} collective-permute-done((bf16[2,256,128]{2,1,0:T(8,128)(2,1)S(1)}, bf16[2,256,128]{2,1,0:T(8,128)(2,1)S(1)}, u32[]{:S(2)}, u32[]{:S(2)}) %collective-permute-start.5) | collective-permute-done | bytes 131104 | tf_op jit(solution)/shard_map/ppermute | solution.py:18
  41.1 1.3 %shard_map.122 = (f32[896,128]{1,0:T(8,128)S(1)}, f32[896,128]{1,0:T(8,128)S(1)}, f32[896,128]{1,0:T(8,128)S(1)}) custom-call(s32[1]{0:T(128)} %bitcast.rank_ref.refs_0_, bf16[896,128]{1,0:T(8,128)(2,1)S(1)} %shard_map.120.refs_1_, f32[8,128]{1,0:T(8,128)S(1)} %get-tuple-element.43.refs_2_, f32[128,1]{1,0:T(8,128)S(1)} %get-tuple-element.44.refs_3_, ...), custom_call_target="tpu_custom_call" | custom-call | flops 469762048 | bytes 7340032 | tf_op jit(solution)/shard_map/pallas_call | solution.py:259
  42.4 5.1 %collective-permute-done.6.refs_8_ = bf16[2,256,128]{2,1,0:T(8,128)(2,1)S(1)} collective-permute-done((bf16[2,256,128]{2,1,0:T(8,128)(2,1)S(1)}, bf16[2,256,128]{2,1,0:T(8,128)(2,1)S(1)}, u32[]{:S(2)}, u32[]{:S(2)}) %collective-permute-start.6) | collective-permute-done | bytes 131104 | tf_op jit(solution)/shard_map/ppermute | solution.py:18
  47.5 0.0 collective-permute-done.7.refs_9_
  47.5 2.3 %shard_map.124 = (f32[896,128]{1,0:T(8,128)S(1)}, f32[896,128]{1,0:T(8,128)S(1)}, f32[896,128]{1,0:T(8,128)S(1)}) custom-call(s32[1]{0:T(128)} %bitcast.rank_ref.refs_0_, bf16[896,128]{1,0:T(8,128)(2,1)S(1)} %shard_map.120.refs_1_, f32[8,128]{1,0:T(8,128)S(1)} %get-tuple-element.43.refs_2_, f32[128,1]{1,0:T(8,128)S(1)} %get-tuple-element.44.refs_3_, ...), custom_call_target="tpu_custom_call" | custom-call | flops 645922816 | bytes 10092544 | tf_op jit(solution)/shard_map/pallas_call | solution.py:259
  49.8 0.0 collective-permute-done.13.refs_9_
  49.8 0.0 collective-permute-done.12.refs_8_
  49.8 2.1 %shard_map.127 = bf16[128,896]{1,0:T(8,128)(2,1)} custom-call(s32[1]{0:T(128)} %bitcast.rank_ref.refs_0_, bf16[896,128]{1,0:T(8,128)(2,1)S(1)} %shard_map.120.refs_1_, f32[8,128]{1,0:T(8,128)S(1)} %get-tuple-element.43.refs_2_, f32[128,1]{1,0:T(8,128)S(1)} %get-tuple-element.44.refs_3_, f32[128,1]{1,0:T(8,128)S(1)} %get-tuple-element.45.refs_4_, ...), custom_call_target="tpu_custom_call" | custom-call | flops 293601280 | bytes 4587520 | tf_op jit(solution)/shard_map/pallas_call | solution.py:259
  (3 shorter events, 0.0 us)
Async XLA Ops:
  0.0 8.8 %collective-permute-start.1 = (bf16[128,896]{1,0:T(8,128)(2,1)}, bf16[128,896]{1,0:T(8,128)(2,1)S(1)}, u32[]{:S(2)}, u32[]{:S(2)}) collective-permute-start(bf16[128,896]{1,0:T(8,128)(2,1)} %refs_0_.1), channel_id=1, source_target_pairs={{0,2},{1,3},{2,0},{3,1},{4,6},{5,7},{6,4},{7,5},{8,10},{9,11},{10,... | collective-permute-start | bytes 688136 | tf_op jit(solution)/shard_map/ppermute | solution.py:18
  3.0 22.3 %collective-permute-start = (bf16[128,896]{1,0:T(8,128)(2,1)}, bf16[128,896]{1,0:T(8,128)(2,1)S(1)}, u32[]{:S(2)}, u32[]{:S(2)}) collective-permute-start(bf16[128,896]{1,0:T(8,128)(2,1)} %refs_0_.1), channel_id=1, source_target_pairs={{0,1},{1,0},{2,3},{3,2},{4,5},{5,4},{6,7},{7,6},{8,9},{9,8},{10,11... | collective-permute-start | bytes 688136 | tf_op jit(solution)/shard_map/ppermute | solution.py:18
  8.8 16.5 %collective-permute-start.2 = (bf16[128,896]{1,0:T(8,128)(2,1)S(1)}, bf16[128,896]{1,0:T(8,128)(2,1)S(1)}, u32[]{:S(2)}, u32[]{:S(2)}) collective-permute-start(bf16[128,896]{1,0:T(8,128)(2,1)S(1)} %collective-permute-done.1.refs_3_), channel_id=1, source_target_pairs={{0,1},{1,0},{2,3},{3,2},{4,5},{5,4},{6,7},{7,6},{8,9},{9,8},{10,11... | collective-permute-start | bytes 688136 | tf_op jit(solution)/shard_map/ppermute | solution.py:18
  9.7 9.9 %collective-permute-start.4 = (bf16[2,256,128]{2,1,0:T(8,128)(2,1)S(1)}, bf16[2,256,128]{2,1,0:T(8,128)(2,1)S(1)}, u32[]{:S(2)}, u32[]{:S(2)}) collective-permute-start(bf16[2,256,128]{2,1,0:T(8,128)(2,1)S(1)} %shard_map.121.refs_5_), channel_id=1, source_target_pairs={{0,16},{4,20},{8,24},{12,28},{16,0},{20,4},{24,8},{28,12},{1,17},{... | collective-permute-start | bytes 393224 | tf_op jit(solution)/shard_map/ppermute | solution.py:18
  19.6 13.4 %collective-permute-start.8 = (bf16[2,256,128]{2,1,0:T(8,128)(2,1)S(1)}, bf16[2,256,128]{2,1,0:T(8,128)(2,1)S(1)}, u32[]{:S(2)}, u32[]{:S(2)}) collective-permute-start(bf16[2,256,128]{2,1,0:T(8,128)(2,1)S(1)} %collective-permute-done.4.refs_7_.refs_1_), channel_id=1, source_target_pairs={{0,8},{4,12},{8,0},{12,4},{16,24},{20,28},{24,16},{28,20},{1,9},{5... | collective-permute-start | bytes 393224 | tf_op jit(solution)/shard_map/ppermute | solution.py:18
  20.3 14.7 %collective-permute-start.3 = (bf16[2,256,128]{2,1,0:T(8,128)(2,1)S(1)}, bf16[2,256,128]{2,1,0:T(8,128)(2,1)S(1)}, u32[]{:S(2)}, u32[]{:S(2)}) collective-permute-start(bf16[2,256,128]{2,1,0:T(8,128)(2,1)S(1)} %shard_map.121.refs_5_), channel_id=1, source_target_pairs={{0,8},{4,12},{8,0},{12,4},{16,24},{20,28},{24,16},{28,20},{1,9},{5... | collective-permute-start | bytes 393224 | tf_op jit(solution)/shard_map/ppermute | solution.py:18
  26.3 5.7 %collective-permute-start.10 = (bf16[2,128,128]{2,1,0:T(8,128)(2,1)S(1)}, bf16[2,128,128]{2,1,0:T(8,128)(2,1)S(1)}, u32[]{:S(2)}, u32[]{:S(2)}) collective-permute-start(bf16[2,128,128]{2,1,0:T(8,128)(2,1)S(1)} %get-tuple-element.49.refs_0_.refs_11_), channel_id=1, source_target_pairs={{0,16},{4,20},{8,24},{12,28},{16,0},{20,4},{24,8},{28,12},{1,17},{... | collective-permute-start | bytes 196616 | tf_op jit(solution)/shard_map/ppermute | solution.py:18
  28.4 6.0 %collective-permute-start.9 = (bf16[2,128,128]{2,1,0:T(8,128)(2,1)S(1)}, bf16[2,128,128]{2,1,0:T(8,128)(2,1)S(1)}, u32[]{:S(2)}, u32[]{:S(2)}) collective-permute-start(bf16[2,128,128]{2,1,0:T(8,128)(2,1)S(1)} %get-tuple-element.49.refs_0_.refs_11_), channel_id=1, source_target_pairs={{0,8},{4,12},{8,0},{12,4},{16,24},{20,28},{24,16},{28,20},{1,9},{5... | collective-permute-start | bytes 196616 | tf_op jit(solution)/shard_map/ppermute | solution.py:18
  30.5 17.1 %collective-permute-start.7 = (bf16[2,384,128]{2,1,0:T(8,128)(2,1)S(1)}, bf16[2,384,128]{2,1,0:T(8,128)(2,1)S(1)}, u32[]{:S(2)}, u32[]{:S(2)}) collective-permute-start(bf16[2,384,128]{2,1,0:T(8,128)(2,1)S(1)} %shard_map.123), channel_id=1, source_target_pairs={{0,4},{4,0},{8,12},{12,8},{16,20},{20,16},{24,28},{28,24},{1,5},{5... | collective-permute-start | bytes 589832 | tf_op jit(solution)/shard_map/ppermute | solution.py:18
  32.0 4.5 %collective-permute-start.11 = (bf16[2,128,128]{2,1,0:T(8,128)(2,1)S(1)}, bf16[2,128,128]{2,1,0:T(8,128)(2,1)S(1)}, u32[]{:S(2)}, u32[]{:S(2)}) collective-permute-start(bf16[2,128,128]{2,1,0:T(8,128)(2,1)S(1)} %collective-permute-done.10.refs_13_.refs_0_), channel_id=1, source_target_pairs={{0,8},{4,12},{8,0},{12,4},{16,24},{20,28},{24,16},{28,20},{1,9},{5... | collective-permute-start | bytes 196616 | tf_op jit(solution)/shard_map/ppermute | solution.py:18
  32.9 8.2 %collective-permute-start.5 = (bf16[2,256,128]{2,1,0:T(8,128)(2,1)S(1)}, bf16[2,256,128]{2,1,0:T(8,128)(2,1)S(1)}, u32[]{:S(2)}, u32[]{:S(2)}) collective-permute-start(bf16[2,256,128]{2,1,0:T(8,128)(2,1)S(1)} %shard_map.121.refs_5_), channel_id=1, source_target_pairs={{0,4},{4,0},{8,12},{12,8},{16,20},{20,16},{24,28},{28,24},{1,5},{5... | collective-permute-start | bytes 393224 | tf_op jit(solution)/shard_map/ppermute | solution.py:18
  34.4 15.4 %collective-permute-start.12 = (bf16[2,384,128]{2,1,0:T(8,128)(2,1)S(1)}, bf16[2,384,128]{2,1,0:T(8,128)(2,1)S(1)}, u32[]{:S(2)}, u32[]{:S(2)}) collective-permute-start(bf16[2,384,128]{2,1,0:T(8,128)(2,1)S(1)} %shard_map.125), channel_id=1, source_target_pairs={{0,4},{4,0},{8,12},{12,8},{16,20},{20,16},{24,28},{28,24},{1,5},{5... | collective-permute-start | bytes 589832 | tf_op jit(solution)/shard_map/ppermute | solution.py:18
  35.0 12.5 %collective-permute-start.6 = (bf16[2,256,128]{2,1,0:T(8,128)(2,1)S(1)}, bf16[2,256,128]{2,1,0:T(8,128)(2,1)S(1)}, u32[]{:S(2)}, u32[]{:S(2)}) collective-permute-start(bf16[2,256,128]{2,1,0:T(8,128)(2,1)S(1)} %collective-permute-done.3.refs_6_), channel_id=1, source_target_pairs={{0,4},{4,0},{8,12},{12,8},{16,20},{20,16},{24,28},{28,24},{1,5},{5... | collective-permute-start | bytes 393224 | tf_op jit(solution)/shard_map/ppermute | solution.py:18
  36.5 13.3 %collective-permute-start.13 = (bf16[2,256,128]{2,1,0:T(8,128)(2,1)S(1)}, bf16[2,256,128]{2,1,0:T(8,128)(2,1)S(1)}, u32[]{:S(2)}, u32[]{:S(2)}) collective-permute-start(bf16[2,256,128]{2,1,0:T(8,128)(2,1)S(1)} %shard_map.126), channel_id=1, source_target_pairs={{0,4},{4,0},{8,12},{12,8},{16,20},{20,16},{24,28},{28,24},{1,5},{5... | collective-permute-start | bytes 393224 | tf_op jit(solution)/shard_map/ppermute | solution.py:18
where the time goes:
time: 52.1 us; the launch traced here: 51.9 us
  waiting for transfers between devices  19.9 us (38%)
  starting transfers between devices  19.3 us (37%)
  Pallas kernels  12.7 us (24%)
    ppermute x14, waiting for transfers between devices, swap(): return lax.ppermute(x, axis, [(i, i ^ k) for i in range(n)])  19.9 us
    ppermute x14, starting transfers between devices, swap(): return lax.ppermute(x, axis, [(i, i ^ k) for i in range(n)])  19.3 us
    pallas_call x10, Pallas kernels, call(): pl.pallas_call(kernel, out_shape=list(outs) if many else outs, in_specs=s...  12.7 us
  transfers between devices with their start and end apart: 14, of which 4 were waited for; matrix products, arithmetic and copies ran while one was open for 0% of the time, Pallas kernels for 20%

commit v1 on v0

--- a/solution.py
+++ b/solution.py
@@ -394,16 +394,17 @@
     f4 = ctx(fresh, 4)
     f2 = ctx(fresh, 2)
     f6 = ctx(f4, 2)
-    ux = ctx(join((fresh, 0, new), (c4, 0, old)), 1)
-    xa = ctx(join((f2, 0, new), (c6, 0, old)), 1)
-    xb = ctx(join((f4, 0, new), (f6, 0, new)), 1)
+    ux = ctx(join((fresh, 0, new), (c6, 0, old)), 1)
+    c5 = ctx(c4, 1)
+    xa = ctx(join((f2, 0, new), (f4, 0, new)), 1)
+    xb = ctx(f6, 1)
     state = attend([(c, 0, old, None) for c in (cache, c2, c4, c1)])
     state = attend(
-        [(c3, 0, old, None), (ux, new, old, None), (c6, 0, old, None)]
+        [(c3, 0, old, None), (c5, 0, old, None), (c6, 0, old, None), (ux, new, old, None)]
         + [(fresh, 0, new, 0), (ux, 0, new, 1), (f2, 0, new, 2), (f4, 0, new, 4), (f6, 0, new, 6)],
         state,
     )
-    return attend([(xa, new, old, None), (xa, 0, new, 3), (xb, 0, new, 5), (xb, new, new, 7)], state, True)
+    return attend([(xa, 0, new, 3), (xa, new, new, 5), (xb, 0, new, 7)], state, True)
 
 
 def paired(n_ctx):

time: 52.1 us -> 40.3 us (0.77)
  waiting for transfers between devices: 19.9 us -> 9.52 us
  starting transfers between devices: 19.3 us -> 18.3 us
    ppermute x14 -> x15, waiting for transfers between devices: 19.9 us -> 9.52 us  [swap(): return lax.ppermute(x, axis, [(i, i ^ k) for i in range(n)])]
    ppermute x14 -> x15, starting transfers between devices: 19.3 us -> 18.3 us  [swap(): return lax.ppermute(x, axis, [(i, i ^ k) for i in range(n)])]
    pallas_call x10 -> x9, Pallas kernels: 12.7 us -> 12.2 us  [call(): pl.pallas_call(kernel, out_shape=list(outs) if many else outs, in_specs=s...]
  transfers between devices with their start and end apart: 14 -> 15, of which waited for: 4 -> 5; matrix products, arithmetic and copies ran while one was open for 0% -> 0% of each run, Pallas kernels for 20% -> 27%
where the time goes in v1:
time: 40.3 us; the launch traced here: 40.1 us
  starting transfers between devices  18.3 us (45%)
  Pallas kernels  12.2 us (30%)
  waiting for transfers between devices  9.52 us (24%)
    ppermute x15, starting transfers between devices, swap(): return lax.ppermute(x, axis, [(i, i ^ k) for i in range(n)])  18.3 us
    pallas_call x9, Pallas kernels, call(): pl.pallas_call(kernel, out_shape=list(outs) if many else outs, in_specs=s...  12.2 us
    ppermute x15, waiting for transfers between devices, swap(): return lax.ppermute(x, axis, [(i, i ^ k) for i in range(n)])  9.52 us
  transfers between devices with their start and end apart: 15, of which 5 were waited for; matrix products, arithmetic and copies ran while one was open for 0% of the time, Pallas kernels for 27%

profile of v1, /device:TPU:0, one launch (start us, length us, event | category | flops | bytes accessed | tf_op | source)
XLA Modules:
  0.0 40.1 jit_solution(12682211776786917609)
XLA Ops:
  0.0 3.0 %collective-permute-start.1 = (bf16[128,896]{1,0:T(8,128)(2,1)}, bf16[128,896]{1,0:T(8,128)(2,1)S(1)}, u32[]{:S(2)}, u32[]{:S(2)}) collective-permute-start(bf16[128,896]{1,0:T(8,128)(2,1)} %refs_0_.1), channel_id=1, source_target_pairs={{0,2},{1,3},{2,0},{3,1},{4,6},{5,7},{6,4},{7,5},{8,10},{9,11},{10,... | collective-permute-start | bytes 688136 | tf_op jit(solution)/shard_map/ppermute | solution.py:18
  3.0 0.9 %shard_map.121.refs_5_ = bf16[2,256,128]{2,1,0:T(8,128)(2,1)S(1)} custom-call(bf16[256,128]{1,0:T(8,128)(2,1)} %key_in.1, bf16[256,128]{1,0:T(8,128)(2,1)} %value_in.1), custom_call_target="tpu_custom_call" | custom-call | bytes 1000000 | tf_op jit(solution)/shard_map/pallas_call | solution.py:259
  3.9 2.7 %collective-permute-start.4 = (bf16[2,256,128]{2,1,0:T(8,128)(2,1)S(1)}, bf16[2,256,128]{2,1,0:T(8,128)(2,1)S(1)}, u32[]{:S(2)}, u32[]{:S(2)}) collective-permute-start(bf16[2,256,128]{2,1,0:T(8,128)(2,1)S(1)} %shard_map.121.refs_5_), channel_id=1, source_target_pairs={{0,16},{4,20},{8,24},{12,28},{16,0},{20,4},{24,8},{28,12},{1,17},{... | collective-permute-start | bytes 393224 | tf_op jit(solution)/shard_map/ppermute | solution.py:18
  6.5 0.0 collective-permute-start
  6.5 2.3 %collective-permute-done.1.refs_3_ = bf16[128,896]{1,0:T(8,128)(2,1)S(1)} collective-permute-done((bf16[128,896]{1,0:T(8,128)(2,1)}, bf16[128,896]{1,0:T(8,128)(2,1)S(1)}, u32[]{:S(2)}, u32[]{:S(2)}) %collective-permute-start.1) | collective-permute-done | bytes 229408 | tf_op jit(solution)/shard_map/ppermute | solution.py:18
  8.8 0.0 collective-permute-start.2
  8.8 3.8 %collective-permute-done.4.refs_7_ = bf16[2,256,128]{2,1,0:T(8,128)(2,1)S(1)} collective-permute-done((bf16[2,256,128]{2,1,0:T(8,128)(2,1)S(1)}, bf16[2,256,128]{2,1,0:T(8,128)(2,1)S(1)}, u32[]{:S(2)}, u32[]{:S(2)}) %collective-permute-start.4) | collective-permute-done | bytes 131104 | tf_op jit(solution)/shard_map/ppermute | solution.py:18
  12.6 0.7 %collective-permute-start.8 = (bf16[2,256,128]{2,1,0:T(8,128)(2,1)S(1)}, bf16[2,256,128]{2,1,0:T(8,128)(2,1)S(1)}, u32[]{:S(2)}, u32[]{:S(2)}) collective-permute-start(bf16[2,256,128]{2,1,0:T(8,128)(2,1)S(1)} %collective-permute-done.4.refs_7_), channel_id=1, source_target_pairs={{0,8},{4,12},{8,0},{12,4},{16,24},{20,28},{24,16},{28,20},{1,9},{5... | collective-permute-start | bytes 393224 | tf_op jit(solution)/shard_map/ppermute | solution.py:18
  13.3 1.4 %collective-permute-start.3 = (bf16[2,256,128]{2,1,0:T(8,128)(2,1)S(1)}, bf16[2,256,128]{2,1,0:T(8,128)(2,1)S(1)}, u32[]{:S(2)}, u32[]{:S(2)}) collective-permute-start(bf16[2,256,128]{2,1,0:T(8,128)(2,1)S(1)} %shard_map.121.refs_5_), channel_id=1, source_target_pairs={{0,8},{4,12},{8,0},{12,4},{16,24},{20,28},{24,16},{28,20},{1,9},{5... | collective-permute-start | bytes 393224 | tf_op jit(solution)/shard_map/ppermute | solution.py:18
  14.6 1.5 %collective-permute-start.5 = (bf16[2,256,128]{2,1,0:T(8,128)(2,1)S(1)}, bf16[2,256,128]{2,1,0:T(8,128)(2,1)S(1)}, u32[]{:S(2)}, u32[]{:S(2)}) collective-permute-start(bf16[2,256,128]{2,1,0:T(8,128)(2,1)S(1)} %shard_map.121.refs_5_), channel_id=1, source_target_pairs={{0,4},{4,0},{8,12},{12,8},{16,20},{20,16},{24,28},{28,24},{1,5},{5... | collective-permute-start | bytes 393224 | tf_op jit(solution)/shard_map/ppermute | solution.py:18
  16.1 3.7 %shard_map.118 = (bf16[128,896]{1,0:T(8,128)(2,1)S(1)}, f32[28,128]{1,0:T(8,128)S(1)}, bf16[3584,128]{1,0:T(8,128)(2,1)S(1)}, f32[1,128]{1,0:T(1,128)S(1)}, bf16...) custom-call(s32[1]{0:T(128)} %bitcast.rank_ref.refs_0_, ...), custom_call_target="tpu_custom_call" | custom-call | bytes 4000000 | tf_op jit(solution)/shard_map/pallas_call | solution.py:259
  19.9 0.0 collective-permute-done.refs_2_
  19.9 0.0 collective-permute-done.2.refs_4_
  19.9 0.9 %shard_map.119 = (bf16[128,3584]{1,0:T(8,128)(2,1)S(1)}, bf16[2,128,128]{2,1,0:T(8,128)(2,1)S(1)}) custom-call(s32[1]{0:T(128)} %bitcast.1.me_ref.refs_0_, bf16[128,896]{1,0:T(8,128)(2,1)S(1)} %get-tuple-element.29.refs_1_, bf16[128,896]{1,0:T(8,128)(2,1)S(1)} %collective-permute-done.refs_2_, bf16[128,896]{1,0:T(8,128)(2,1)S(1)} %collective-permute-done.1.refs_3_, ...), custom_call_target="tpu_custom_call" | custom-call | flops 234881024 | bytes 3000000 | tf_op jit(solution)/shard_map/pallas_call | solution.py:259
  20.8 0.7 %collective-permute-start.10 = (bf16[2,128,128]{2,1,0:T(8,128)(2,1)S(1)}, bf16[2,128,128]{2,1,0:T(8,128)(2,1)S(1)}, u32[]{:S(2)}, u32[]{:S(2)}) collective-permute-start(bf16[2,128,128]{2,1,0:T(8,128)(2,1)S(1)} %get-tuple-element.49.refs_0_.refs_12_), channel_id=1, source_target_pairs={{0,8},{4,12},{8,0},{12,4},{16,24},{20,28},{24,16},{28,20},{1,9},{5... | collective-permute-start | bytes 196616 | tf_op jit(solution)/shard_map/ppermute | solution.py:18
  21.6 0.0 collective-permute-done.8.refs_1_.refs_10_
  21.6 0.6 %collective-permute-start.9 = (bf16[2,384,128]{2,1,0:T(8,128)(2,1)S(1)}, bf16[2,384,128]{2,1,0:T(8,128)(2,1)S(1)}, u32[]{:S(2)}, u32[]{:S(2)}) collective-permute-start(bf16[2,384,128]{2,1,0:T(8,128)(2,1)S(1)} %shard_map.123), channel_id=1, source_target_pairs={{0,4},{4,0},{8,12},{12,8},{16,20},{20,16},{24,28},{28,24},{1,5},{5... | collective-permute-start | bytes 589832 | tf_op jit(solution)/shard_map/ppermute | solution.py:18
  22.2 3.4 %collective-permute-start.11 = (bf16[2,128,128]{2,1,0:T(8,128)(2,1)S(1)}, bf16[2,128,128]{2,1,0:T(8,128)(2,1)S(1)}, u32[]{:S(2)}, u32[]{:S(2)}) collective-permute-start(bf16[2,128,128]{2,1,0:T(8,128)(2,1)S(1)} %get-tuple-element.49.refs_0_.refs_12_), channel_id=1, source_target_pairs={{0,16},{4,20},{8,24},{12,28},{16,0},{20,4},{24,8},{28,12},{1,17},{... | collective-permute-start | bytes 196616 | tf_op jit(solution)/shard_map/ppermute | solution.py:18
  25.6 0.0 collective-permute-done.3.refs_6_
  25.6 1.5 %collective-permute-start.7 = (bf16[2,256,128]{2,1,0:T(8,128)(2,1)S(1)}, bf16[2,256,128]{2,1,0:T(8,128)(2,1)S(1)}, u32[]{:S(2)}, u32[]{:S(2)}) collective-permute-start(bf16[2,256,128]{2,1,0:T(8,128)(2,1)S(1)} %collective-permute-done.4.refs_7_), channel_id=1, source_target_pairs={{0,4},{4,0},{8,12},{12,8},{16,20},{20,16},{24,28},{28,24},{1,5},{5... | collective-permute-start | bytes 393224 | tf_op jit(solution)/shard_map/ppermute | solution.py:18
  27.1 0.0 collective-permute-done.10.refs_13_.refs_0_
  27.1 0.5 %collective-permute-start.6 = (bf16[2,256,128]{2,1,0:T(8,128)(2,1)S(1)}, bf16[2,256,128]{2,1,0:T(8,128)(2,1)S(1)}, u32[]{:S(2)}, u32[]{:S(2)}) collective-permute-start(bf16[2,256,128]{2,1,0:T(8,128)(2,1)S(1)} %collective-permute-done.3.refs_6_), channel_id=1, source_target_pairs={{0,4},{4,0},{8,12},{12,8},{16,20},{20,16},{24,28},{28,24},{1,5},{5... | collective-permute-start | bytes 393224 | tf_op jit(solution)/shard_map/ppermute | solution.py:18
  27.6 0.9 %collective-permute-done.11.refs_14_.refs_1_ = bf16[2,128,128]{2,1,0:T(8,128)(2,1)S(1)} collective-permute-done((bf16[2,128,128]{2,1,0:T(8,128)(2,1)S(1)}, bf16[2,128,128]{2,1,0:T(8,128)(2,1)S(1)}, u32[]{:S(2)}, u32[]{:S(2)}) %collective-permute-start.11) | collective-permute-done | bytes 65568 | tf_op jit(solution)/shard_map/ppermute | solution.py:18
  28.5 1.6 %collective-permute-start.13 = (bf16[2,256,128]{2,1,0:T(8,128)(2,1)S(1)}, bf16[2,256,128]{2,1,0:T(8,128)(2,1)S(1)}, u32[]{:S(2)}, u32[]{:S(2)}) collective-permute-start(bf16[2,256,128]{2,1,0:T(8,128)(2,1)S(1)} %shard_map.125), channel_id=1, source_target_pairs={{0,4},{4,0},{8,12},{12,8},{16,20},{20,16},{24,28},{28,24},{1,5},{5... | collective-permute-start | bytes 393224 | tf_op jit(solution)/shard_map/ppermute | solution.py:18
  30.1 0.0 collective-permute-done.5.refs_8_
  30.1 0.3 collective-permute-start.12
  30.4 1.4 %shard_map.120.refs_1_ = bf16[896,128]{1,0:T(8,128)(2,1)S(1)} custom-call(s32[1]{0:T(128)} %bitcast.1.me_ref.refs_0_, bf16[128,3584]{1,0:T(8,128)(2,1)S(1)} %get-tuple-element.37.normed, f32[7,128]{1,0:T(8,128)S(1)} %get-tuple-element.38.bias_query, f32[128,128]{1,0:T(8,128)S(1)} %get-tuple-element.35.refs_10_.cosine, ...), custom_call_target="tpu_custom_call" | custom-call | flops 822083584 | bytes 7000000 | tf_op jit(solution)/shard_map/pallas_call | solution.py:259
  31.8 1.3 %shard_map.122 = (f32[896,128]{1,0:T(8,128)S(1)}, f32[896,128]{1,0:T(8,128)S(1)}, f32[896,128]{1,0:T(8,128)S(1)}) custom-call(s32[1]{0:T(128)} %bitcast.rank_ref.refs_0_, bf16[896,128]{1,0:T(8,128)(2,1)S(1)} %shard_map.120.refs_1_, f32[8,128]{1,0:T(8,128)S(1)} %get-tuple-element.43.refs_2_, f32[128,1]{1,0:T(8,128)S(1)} %get-tuple-element.44.refs_3_, ...), custom_call_target="tpu_custom_call" | custom-call | flops 469762048 | bytes 7340032 | tf_op jit(solution)/shard_map/pallas_call | solution.py:259
  33.1 1.2 %collective-permute-done.12.refs_15_ = bf16[2,128,128]{2,1,0:T(8,128)(2,1)S(1)} collective-permute-done((bf16[2,128,128]{2,1,0:T(8,128)(2,1)S(1)}, bf16[2,128,128]{2,1,0:T(8,128)(2,1)S(1)}, u32[]{:S(2)}, u32[]{:S(2)}) %collective-permute-start.12) | collective-permute-done | bytes 65568 | tf_op jit(solution)/shard_map/ppermute | solution.py:18
  34.3 0.5 %collective-permute-start.14 = (bf16[2,128,128]{2,1,0:T(8,128)(2,1)S(1)}, bf16[2,128,128]{2,1,0:T(8,128)(2,1)S(1)}, u32[]{:S(2)}, u32[]{:S(2)}) collective-permute-start(bf16[2,128,128]{2,1,0:T(8,128)(2,1)S(1)} %collective-permute-done.12.refs_15_), channel_id=1, source_target_pairs={{0,4},{4,0},{8,12},{12,8},{16,20},{20,16},{24,28},{28,24},{1,5},{5... | collective-permute-start | bytes 196616 | tf_op jit(solution)/shard_map/ppermute | solution.py:18
  34.9 0.0 collective-permute-done.7.refs_9_
  34.9 0.0 collective-permute-done.6.refs_8_
  34.9 0.0 collective-permute-done.9.refs_11_
  34.9 2.4 %shard_map.124 = (f32[896,128]{1,0:T(8,128)S(1)}, f32[896,128]{1,0:T(8,128)S(1)}, f32[896,128]{1,0:T(8,128)S(1)}) custom-call(s32[1]{0:T(128)} %bitcast.rank_ref.refs_0_, bf16[896,128]{1,0:T(8,128)(2,1)S(1)} %shard_map.120.refs_1_, f32[8,128]{1,0:T(8,128)S(1)} %get-tuple-element.43.refs_2_, f32[128,1]{1,0:T(8,128)S(1)} %get-tuple-element.44.refs_3_, ...), custom_call_target="tpu_custom_call" | custom-call | flops 763363328 | bytes 11927552 | tf_op jit(solution)/shard_map/pallas_call | solution.py:259
  37.3 1.3 %collective-permute-done.14.refs_9_ = bf16[2,128,128]{2,1,0:T(8,128)(2,1)S(1)} collective-permute-done((bf16[2,128,128]{2,1,0:T(8,128)(2,1)S(1)}, bf16[2,128,128]{2,1,0:T(8,128)(2,1)S(1)}, u32[]{:S(2)}, u32[]{:S(2)}) %collective-permute-start.14) | collective-permute-done | bytes 65568 | tf_op jit(solution)/shard_map/ppermute | solution.py:18
  38.6 0.0 collective-permute-done.13.refs_8_
  38.6 1.5 %shard_map.126 = bf16[128,896]{1,0:T(8,128)(2,1)} custom-call(s32[1]{0:T(128)} %bitcast.rank_ref.refs_0_, bf16[896,128]{1,0:T(8,128)(2,1)S(1)} %shard_map.120.refs_1_, f32[8,128]{1,0:T(8,128)S(1)} %get-tuple-element.43.refs_2_, f32[128,1]{1,0:T(8,128)S(1)} %get-tuple-element.44.refs_3_, f32[128,1]{1,0:T(8,128)S(1)} %get-tuple-element.45.refs_4_, ...), custom_call_target="tpu_custom_call" | custom-call | flops 176160768 | bytes 2752512 | tf_op jit(solution)/shard_map/pallas_call | solution.py:259
  (2 shorter events, 0.0 us)
Async XLA Ops:
  0.0 8.8 %collective-permute-start.1 = (bf16[128,896]{1,0:T(8,128)(2,1)}, bf16[128,896]{1,0:T(8,128)(2,1)S(1)}, u32[]{:S(2)}, u32[]{:S(2)}) collective-permute-start(bf16[128,896]{1,0:T(8,128)(2,1)} %refs_0_.1), channel_id=1, source_target_pairs={{0,2},{1,3},{2,0},{3,1},{4,6},{5,7},{6,4},{7,5},{8,10},{9,11},{10,... | collective-permute-start | bytes 688136 | tf_op jit(solution)/shard_map/ppermute | solution.py:18
  3.9 8.7 %collective-permute-start.4 = (bf16[2,256,128]{2,1,0:T(8,128)(2,1)S(1)}, bf16[2,256,128]{2,1,0:T(8,128)(2,1)S(1)}, u32[]{:S(2)}, u32[]{:S(2)}) collective-permute-start(bf16[2,256,128]{2,1,0:T(8,128)(2,1)S(1)} %shard_map.121.refs_5_), channel_id=1, source_target_pairs={{0,16},{4,20},{8,24},{12,28},{16,0},{20,4},{24,8},{28,12},{1,17},{... | collective-permute-start | bytes 393224 | tf_op jit(solution)/shard_map/ppermute | solution.py:18
  6.5 13.3 %collective-permute-start = (bf16[128,896]{1,0:T(8,128)(2,1)}, bf16[128,896]{1,0:T(8,128)(2,1)S(1)}, u32[]{:S(2)}, u32[]{:S(2)}) collective-permute-start(bf16[128,896]{1,0:T(8,128)(2,1)} %refs_0_.1), channel_id=1, source_target_pairs={{0,1},{1,0},{2,3},{3,2},{4,5},{5,4},{6,7},{7,6},{8,9},{9,8},{10,11... | collective-permute-start | bytes 688136 | tf_op jit(solution)/shard_map/ppermute | solution.py:18
  8.8 11.1 %collective-permute-start.2 = (bf16[128,896]{1,0:T(8,128)(2,1)S(1)}, bf16[128,896]{1,0:T(8,128)(2,1)S(1)}, u32[]{:S(2)}, u32[]{:S(2)}) collective-permute-start(bf16[128,896]{1,0:T(8,128)(2,1)S(1)} %collective-permute-done.1.refs_3_), channel_id=1, source_target_pairs={{0,1},{1,0},{2,3},{3,2},{4,5},{5,4},{6,7},{7,6},{8,9},{9,8},{10,11... | collective-permute-start | bytes 688136 | tf_op jit(solution)/shard_map/ppermute | solution.py:18
  12.6 8.9 %collective-permute-start.8 = (bf16[2,256,128]{2,1,0:T(8,128)(2,1)S(1)}, bf16[2,256,128]{2,1,0:T(8,128)(2,1)S(1)}, u32[]{:S(2)}, u32[]{:S(2)}) collective-permute-start(bf16[2,256,128]{2,1,0:T(8,128)(2,1)S(1)} %collective-permute-done.4.refs_7_), channel_id=1, source_target_pairs={{0,8},{4,12},{8,0},{12,4},{16,24},{20,28},{24,16},{28,20},{1,9},{5... | collective-permute-start | bytes 393224 | tf_op jit(solution)/shard_map/ppermute | solution.py:18
  13.3 12.3 %collective-permute-start.3 = (bf16[2,256,128]{2,1,0:T(8,128)(2,1)S(1)}, bf16[2,256,128]{2,1,0:T(8,128)(2,1)S(1)}, u32[]{:S(2)}, u32[]{:S(2)}) collective-permute-start(bf16[2,256,128]{2,1,0:T(8,128)(2,1)S(1)} %shard_map.121.refs_5_), channel_id=1, source_target_pairs={{0,8},{4,12},{8,0},{12,4},{16,24},{20,28},{24,16},{28,20},{1,9},{5... | collective-permute-start | bytes 393224 | tf_op jit(solution)/shard_map/ppermute | solution.py:18
  14.6 15.4 %collective-permute-start.5 = (bf16[2,256,128]{2,1,0:T(8,128)(2,1)S(1)}, bf16[2,256,128]{2,1,0:T(8,128)(2,1)S(1)}, u32[]{:S(2)}, u32[]{:S(2)}) collective-permute-start(bf16[2,256,128]{2,1,0:T(8,128)(2,1)S(1)} %shard_map.121.refs_5_), channel_id=1, source_target_pairs={{0,4},{4,0},{8,12},{12,8},{16,20},{20,16},{24,28},{28,24},{1,5},{5... | collective-permute-start | bytes 393224 | tf_op jit(solution)/shard_map/ppermute | solution.py:18
  20.8 6.2 %collective-permute-start.10 = (bf16[2,128,128]{2,1,0:T(8,128)(2,1)S(1)}, bf16[2,128,128]{2,1,0:T(8,128)(2,1)S(1)}, u32[]{:S(2)}, u32[]{:S(2)}) collective-permute-start(bf16[2,128,128]{2,1,0:T(8,128)(2,1)S(1)} %get-tuple-element.49.refs_0_.refs_12_), channel_id=1, source_target_pairs={{0,8},{4,12},{8,0},{12,4},{16,24},{20,28},{24,16},{28,20},{1,9},{5... | collective-permute-start | bytes 196616 | tf_op jit(solution)/shard_map/ppermute | solution.py:18
  21.6 13.3 %collective-permute-start.9 = (bf16[2,384,128]{2,1,0:T(8,128)(2,1)S(1)}, bf16[2,384,128]{2,1,0:T(8,128)(2,1)S(1)}, u32[]{:S(2)}, u32[]{:S(2)}) collective-permute-start(bf16[2,384,128]{2,1,0:T(8,128)(2,1)S(1)} %shard_map.123), channel_id=1, source_target_pairs={{0,4},{4,0},{8,12},{12,8},{16,20},{20,16},{24,28},{28,24},{1,5},{5... | collective-permute-start | bytes 589832 | tf_op jit(solution)/shard_map/ppermute | solution.py:18
  22.2 6.3 %collective-permute-start.11 = (bf16[2,128,128]{2,1,0:T(8,128)(2,1)S(1)}, bf16[2,128,128]{2,1,0:T(8,128)(2,1)S(1)}, u32[]{:S(2)}, u32[]{:S(2)}) collective-permute-start(bf16[2,128,128]{2,1,0:T(8,128)(2,1)S(1)} %get-tuple-element.49.refs_0_.refs_12_), channel_id=1, source_target_pairs={{0,16},{4,20},{8,24},{12,28},{16,0},{20,4},{24,8},{28,12},{1,17},{... | collective-permute-start | bytes 196616 | tf_op jit(solution)/shard_map/ppermute | solution.py:18
  25.6 9.3 %collective-permute-start.7 = (bf16[2,256,128]{2,1,0:T(8,128)(2,1)S(1)}, bf16[2,256,128]{2,1,0:T(8,128)(2,1)S(1)}, u32[]{:S(2)}, u32[]{:S(2)}) collective-permute-start(bf16[2,256,128]{2,1,0:T(8,128)(2,1)S(1)} %collective-permute-done.4.refs_7_), channel_id=1, source_target_pairs={{0,4},{4,0},{8,12},{12,8},{16,20},{20,16},{24,28},{28,24},{1,5},{5... | collective-permute-start | bytes 393224 | tf_op jit(solution)/shard_map/ppermute | solution.py:18
  27.1 7.8 %collective-permute-start.6 = (bf16[2,256,128]{2,1,0:T(8,128)(2,1)S(1)}, bf16[2,256,128]{2,1,0:T(8,128)(2,1)S(1)}, u32[]{:S(2)}, u32[]{:S(2)}) collective-permute-start(bf16[2,256,128]{2,1,0:T(8,128)(2,1)S(1)} %collective-permute-done.3.refs_6_), channel_id=1, source_target_pairs={{0,4},{4,0},{8,12},{12,8},{16,20},{20,16},{24,28},{28,24},{1,5},{5... | collective-permute-start | bytes 393224 | tf_op jit(solution)/shard_map/ppermute | solution.py:18
  28.5 10.1 %collective-permute-start.13 = (bf16[2,256,128]{2,1,0:T(8,128)(2,1)S(1)}, bf16[2,256,128]{2,1,0:T(8,128)(2,1)S(1)}, u32[]{:S(2)}, u32[]{:S(2)}) collective-permute-start(bf16[2,256,128]{2,1,0:T(8,128)(2,1)S(1)} %shard_map.125), channel_id=1, source_target_pairs={{0,4},{4,0},{8,12},{12,8},{16,20},{20,16},{24,28},{28,24},{1,5},{5... | collective-permute-start | bytes 393224 | tf_op jit(solution)/shard_map/ppermute | solution.py:18
  30.1 4.3 %collective-permute-start.12 = (bf16[2,128,128]{2,1,0:T(8,128)(2,1)S(1)}, bf16[2,128,128]{2,1,0:T(8,128)(2,1)S(1)}, u32[]{:S(2)}, u32[]{:S(2)}) collective-permute-start(bf16[2,128,128]{2,1,0:T(8,128)(2,1)S(1)} %collective-permute-done.11.refs_14_.refs_1_), channel_id=1, source_target_pairs={{0,8},{4,12},{8,0},{12,4},{16,24},{20,28},{24,16},{28,20},{1,9},{5... | collective-permute-start | bytes 196616 | tf_op jit(solution)/shard_map/ppermute | solution.py:18
  34.3 4.3 %collective-permute-start.14 = (bf16[2,128,128]{2,1,0:T(8,128)(2,1)S(1)}, bf16[2,128,128]{2,1,0:T(8,128)(2,1)S(1)}, u32[]{:S(2)}, u32[]{:S(2)}) collective-permute-start(bf16[2,128,128]{2,1,0:T(8,128)(2,1)S(1)} %collective-permute-done.12.refs_15_), channel_id=1, source_target_pairs={{0,4},{4,0},{8,12},{12,8},{16,20},{20,16},{24,28},{28,24},{1,5},{5... | collective-permute-start | bytes 196616 | tf_op jit(solution)/shard_map/ppermute | solution.py:18

commit v2 on v1

--- a/solution.py
+++ b/solution.py
@@ -93,11 +93,18 @@
     return jnp.concatenate([block[i : i + 1] for i in range(count)], axis=1)
 
 
+def stack_rows_kernel(first, second, out):
+    rows = first.shape[0]
+    out[:rows, :] = first[...]
+    out[rows:, :] = second[...]
+
+
 def key_value_kernel(parts, *refs):
     me_ref = refs[0]
-    hidden_refs = refs[1 : 1 + parts]
-    gain, w_key, bias_key, w_value, bias_value, cosine, sine, normed, fresh = refs[1 + parts :]
-    width = hidden_refs[0].shape[1]
+    gain, w_key, bias_key, w_value, bias_value, cosine, sine, normed, fresh = refs[3:]
+    rows = normed.shape[0]
+    hidden_refs = [ref.at[spot : spot + rows, :] for spot in (0, rows) for ref in refs[1:3]]
+    width = normed.shape[1] // parts
     me = me_ref[0]
     square = None
     for ref in hidden_refs:
@@ -177,7 +184,7 @@
     for segment in segments:
         group.append(segment)
         count += segment[2]
-        if count >= CHUNK or segment is segments[-1]:
+        if count >= (CHUNK if segment[3] is None else FRESH) or segment is segments[-1]:
             yield group
             group, count = [], 0
 
@@ -246,6 +253,7 @@
 
 
 CHUNK = 512
+FRESH = 384
 
 
 def call(kernel, outs, args, scalars=0, far=(), scratch=(), flops=0, moved=0):
@@ -291,7 +299,6 @@
     f32, bf16 = jnp.float32, jnp.bfloat16
 
     far_hidden = swap(hidden, "tp", n_tp, 2)
-    pieces = [hidden, swap(hidden, "tp", n_tp, 1), far_hidden, swap(far_hidden, "tp", n_tp, 1)]
 
     carried = (
         hidden,
@@ -332,14 +339,16 @@
         0,
         4000000,
     )
-    pieces[0], gain, key_weight, key_bias, value_weight, value_bias, query_bias = setup[:7]
+    own_hidden, gain, key_weight, key_bias, value_weight, value_bias, query_bias = setup[:7]
     early = setup[7 : 7 + EARLY]
     cosine, sine, tags, own_order, live = setup[7 + EARLY :]
 
+    halves = call(stack_rows_kernel, sds((2 * rows, width), bf16), (own_hidden, far_hidden))
+    beside = swap(halves, "tp", n_tp, 1)
     normed, fresh = call(
         functools.partial(key_value_kernel, n_tp),
         (sds((rows, width * n_tp), bf16), sds((2, rows, kv_width), bf16)),
-        (me, *pieces, gain, key_weight, key_bias, value_weight, value_bias, cosine, sine),
+        (me, halves, beside, gain, key_weight, key_bias, value_weight, value_bias, cosine, sine),
         1,
         flops=2 * rows * width * n_tp * 2 * kv_width,
         moved=3000000,

time: 40.3 us -> 43.9 us (1.089)
  waiting for transfers between devices: 9.52 us -> 11.6 us
  starting transfers between devices: 18.3 us -> 19.9 us
    ppermute x15 -> x14, waiting for transfers between devices: 9.52 us -> 11.6 us  [swap(): return lax.ppermute(x, axis, [(i, i ^ k) for i in range(n)])]
    ppermute x15 -> x14, starting transfers between devices: 18.3 us -> 19.9 us  [swap(): return lax.ppermute(x, axis, [(i, i ^ k) for i in range(n)])]
    pallas_call x9 -> x10, Pallas kernels: 12.2 us -> 12.2 us  [call(): pl.pallas_call(kernel, out_shape=list(outs) if many else outs, in_specs=s...]
  transfers between devices with their start and end apart: 15 -> 14, of which waited for: 5 -> 5; matrix products, arithmetic and copies ran while one was open for 0% -> 0% of each run, Pallas kernels for 27% -> 24%
where the time goes in v2:
time: 43.9 us; the launch traced here: 43.8 us
  starting transfers between devices  19.9 us (45%)
  Pallas kernels  12.2 us (28%)
  waiting for transfers between devices  11.6 us (26%)
    ppermute x14, starting transfers between devices, swap(): return lax.ppermute(x, axis, [(i, i ^ k) for i in range(n)])  19.9 us
    pallas_call x10, Pallas kernels, call(): pl.pallas_call(kernel, out_shape=list(outs) if many else outs, in_specs=s...  12.2 us
    ppermute x14, waiting for transfers between devices, swap(): return lax.ppermute(x, axis, [(i, i ^ k) for i in range(n)])  11.6 us
  transfers between devices with their start and end apart: 14, of which 5 were waited for; matrix products, arithmetic and copies ran while one was open for 0% of the time, Pallas kernels for 24%

profile of v2, /device:TPU:0, one launch (start us, length us, event | category | flops | bytes accessed | tf_op | source)
XLA Modules:
  0.0 43.8 jit_solution(14877852170454731690)
XLA Ops:
  0.0 3.0 %collective-permute-start = (bf16[128,896]{1,0:T(8,128)(2,1)}, bf16[128,896]{1,0:T(8,128)(2,1)S(1)}, u32[]{:S(2)}, u32[]{:S(2)}) collective-permute-start(bf16[128,896]{1,0:T(8,128)(2,1)} %refs_0_.1), channel_id=1, source_target_pairs={{0,2},{1,3},{2,0},{3,1},{4,6},{5,7},{6,4},{7,5},{8,10},{9,11},{10,... | collective-permute-start | bytes 688136 | tf_op jit(solution)/shard_map/ppermute | solution.py:18
  3.0 3.7 %shard_map.118 = (bf16[128,896]{1,0:T(8,128)(2,1)S(1)}, f32[28,128]{1,0:T(8,128)S(1)}, bf16[3584,128]{1,0:T(8,128)(2,1)S(1)}, f32[1,128]{1,0:T(1,128)S(1)}, bf16...) custom-call(s32[1]{0:T(128)} %bitcast.rank_ref.refs_0_, ...), custom_call_target="tpu_custom_call" | custom-call | bytes 4000000 | tf_op jit(solution)/shard_map/pallas_call | solution.py:267
  6.7 2.1 %collective-permute-done.second = bf16[128,896]{1,0:T(8,128)(2,1)S(1)} collective-permute-done((bf16[128,896]{1,0:T(8,128)(2,1)}, bf16[128,896]{1,0:T(8,128)(2,1)S(1)}, u32[]{:S(2)}, u32[]{:S(2)}) %collective-permute-start) | collective-permute-done | bytes 229408 | tf_op jit(solution)/shard_map/ppermute | solution.py:18
  8.8 0.1 collective-permute-start.1
  8.9 0.9 %shard_map.122.refs_5_ = bf16[2,256,128]{2,1,0:T(8,128)(2,1)S(1)} custom-call(bf16[256,128]{1,0:T(8,128)(2,1)} %key_in.1, bf16[256,128]{1,0:T(8,128)(2,1)} %value_in.1), custom_call_target="tpu_custom_call" | custom-call | bytes 1000000 | tf_op jit(solution)/shard_map/pallas_call | solution.py:267
  9.8 2.9 %collective-permute-start.3 = (bf16[2,256,128]{2,1,0:T(8,128)(2,1)S(1)}, bf16[2,256,128]{2,1,0:T(8,128)(2,1)S(1)}, u32[]{:S(2)}, u32[]{:S(2)}) collective-permute-start(bf16[2,256,128]{2,1,0:T(8,128)(2,1)S(1)} %shard_map.122.refs_5_), channel_id=1, source_target_pairs={{0,16},{4,20},{8,24},{12,28},{16,0},{20,4},{24,8},{28,12},{1,17},{... | collective-permute-start | bytes 393224 | tf_op jit(solution)/shard_map/ppermute | solution.py:18
  12.7 7.0 %collective-permute-done.3.refs_7_ = bf16[2,256,128]{2,1,0:T(8,128)(2,1)S(1)} collective-permute-done((bf16[2,256,128]{2,1,0:T(8,128)(2,1)S(1)}, bf16[2,256,128]{2,1,0:T(8,128)(2,1)S(1)}, u32[]{:S(2)}, u32[]{:S(2)}) %collective-permute-start.3) | collective-permute-done | bytes 131104 | tf_op jit(solution)/shard_map/ppermute | solution.py:18
  19.7 0.7 %collective-permute-start.7 = (bf16[2,256,128]{2,1,0:T(8,128)(2,1)S(1)}, bf16[2,256,128]{2,1,0:T(8,128)(2,1)S(1)}, u32[]{:S(2)}, u32[]{:S(2)}) collective-permute-start(bf16[2,256,128]{2,1,0:T(8,128)(2,1)S(1)} %collective-permute-done.3.refs_7_), channel_id=1, source_target_pairs={{0,8},{4,12},{8,0},{12,4},{16,24},{20,28},{24,16},{28,20},{1,9},{5... | collective-permute-start | bytes 393224 | tf_op jit(solution)/shard_map/ppermute | solution.py:18
  20.4 1.3 %collective-permute-start.2 = (bf16[2,256,128]{2,1,0:T(8,128)(2,1)S(1)}, bf16[2,256,128]{2,1,0:T(8,128)(2,1)S(1)}, u32[]{:S(2)}, u32[]{:S(2)}) collective-permute-start(bf16[2,256,128]{2,1,0:T(8,128)(2,1)S(1)} %shard_map.122.refs_5_), channel_id=1, source_target_pairs={{0,8},{4,12},{8,0},{12,4},{16,24},{20,28},{24,16},{28,20},{1,9},{5... | collective-permute-start | bytes 393224 | tf_op jit(solution)/shard_map/ppermute | solution.py:18
  21.7 1.5 %collective-permute-start.4 = (bf16[2,256,128]{2,1,0:T(8,128)(2,1)S(1)}, bf16[2,256,128]{2,1,0:T(8,128)(2,1)S(1)}, u32[]{:S(2)}, u32[]{:S(2)}) collective-permute-start(bf16[2,256,128]{2,1,0:T(8,128)(2,1)S(1)} %shard_map.122.refs_5_), channel_id=1, source_target_pairs={{0,4},{4,0},{8,12},{12,8},{16,20},{20,16},{24,28},{28,24},{1,5},{5... | collective-permute-start | bytes 393224 | tf_op jit(solution)/shard_map/ppermute | solution.py:18
  23.2 0.0 collective-permute-done.1.refs_2_
  23.2 0.9 %shard_map.120 = (bf16[128,3584]{1,0:T(8,128)(2,1)S(1)}, bf16[2,128,128]{2,1,0:T(8,128)(2,1)S(1)}) custom-call(s32[1]{0:T(128)} %bitcast.1.me_ref.refs_0_, bf16[256,896]{1,0:T(8,128)(2,1)S(1)} %shard_map.119.refs_1_, bf16[256,896]{1,0:T(8,128)(2,1)S(1)} %collective-permute-done.1.refs_2_, f32[28,128]{1,0:T(8,128)S(1)} %get-tuple-element.30.refs_3_, ...), custom_call_target="tpu_custom_call" | custom-call | flops 234881024 | bytes 3000000 | tf_op jit(solution)/shard_map/pallas_call | solution.py:267
  24.2 2.1 %collective-permute-start.10 = (bf16[2,128,128]{2,1,0:T(8,128)(2,1)S(1)}, bf16[2,128,128]{2,1,0:T(8,128)(2,1)S(1)}, u32[]{:S(2)}, u32[]{:S(2)}) collective-permute-start(bf16[2,128,128]{2,1,0:T(8,128)(2,1)S(1)} %get-tuple-element.49.refs_0_.refs_12_), channel_id=1, source_target_pairs={{0,16},{4,20},{8,24},{12,28},{16,0},{20,4},{24,8},{28,12},{1,17},{... | collective-permute-start | bytes 196616 | tf_op jit(solution)/shard_map/ppermute | solution.py:18
  26.3 0.0 collective-permute-done.7.refs_1_.refs_10_
  26.3 2.1 %collective-permute-start.8 = (bf16[2,384,128]{2,1,0:T(8,128)(2,1)S(1)}, bf16[2,384,128]{2,1,0:T(8,128)(2,1)S(1)}, u32[]{:S(2)}, u32[]{:S(2)}) collective-permute-start(bf16[2,384,128]{2,1,0:T(8,128)(2,1)S(1)} %shard_map.124), channel_id=1, source_target_pairs={{0,4},{4,0},{8,12},{12,8},{16,20},{20,16},{24,28},{28,24},{1,5},{5... | collective-permute-start | bytes 589832 | tf_op jit(solution)/shard_map/ppermute | solution.py:18
  28.4 0.5 %collective-permute-start.9 = (bf16[2,128,128]{2,1,0:T(8,128)(2,1)S(1)}, bf16[2,128,128]{2,1,0:T(8,128)(2,1)S(1)}, u32[]{:S(2)}, u32[]{:S(2)}) collective-permute-start(bf16[2,128,128]{2,1,0:T(8,128)(2,1)S(1)} %get-tuple-element.49.refs_0_.refs_12_), channel_id=1, source_target_pairs={{0,8},{4,12},{8,0},{12,4},{16,24},{20,28},{24,16},{28,20},{1,9},{5... | collective-permute-start | bytes 196616 | tf_op jit(solution)/shard_map/ppermute | solution.py:18
  28.9 0.0 collective-permute-done.2.refs_6_
  28.9 2.0 %collective-permute-start.6 = (bf16[2,256,128]{2,1,0:T(8,128)(2,1)S(1)}, bf16[2,256,128]{2,1,0:T(8,128)(2,1)S(1)}, u32[]{:S(2)}, u32[]{:S(2)}) collective-permute-start(bf16[2,256,128]{2,1,0:T(8,128)(2,1)S(1)} %collective-permute-done.3.refs_7_), channel_id=1, source_target_pairs={{0,4},{4,0},{8,12},{12,8},{16,20},{20,16},{24,28},{28,24},{1,5},{5... | collective-permute-start | bytes 393224 | tf_op jit(solution)/shard_map/ppermute | solution.py:18
  30.9 0.0 collective-permute-done.10.refs_14_.refs_1_
  30.9 0.0 collective-permute-start.5
  31.0 1.7 %collective-permute-done.9.refs_13_.refs_0_ = bf16[2,128,128]{2,1,0:T(8,128)(2,1)S(1)} collective-permute-done((bf16[2,128,128]{2,1,0:T(8,128)(2,1)S(1)}, bf16[2,128,128]{2,1,0:T(8,128)(2,1)S(1)}, u32[]{:S(2)}, u32[]{:S(2)}) %collective-permute-start.9) | collective-permute-done | bytes 65568 | tf_op jit(solution)/shard_map/ppermute | solution.py:18
  32.6 0.4 collective-permute-start.12
  33.0 0.0 collective-permute-done.4.refs_8_
  33.0 1.7 %collective-permute-start.11 = (bf16[2,128,128]{2,1,0:T(8,128)(2,1)S(1)}, bf16[2,128,128]{2,1,0:T(8,128)(2,1)S(1)}, u32[]{:S(2)}, u32[]{:S(2)}) collective-permute-start(bf16[2,128,128]{2,1,0:T(8,128)(2,1)S(1)} %collective-permute-done.10.refs_14_.refs_1_), channel_id=1, source_target_pairs={{0,8},{4,12},{8,0},{12,4},{16,24},{20,28},{24,16},{28,20},{1,9},{5... | collective-permute-start | bytes 196616 | tf_op jit(solution)/shard_map/ppermute | solution.py:18
  34.7 1.4 %shard_map.121.refs_1_ = bf16[896,128]{1,0:T(8,128)(2,1)S(1)} custom-call(s32[1]{0:T(128)} %bitcast.1.me_ref.refs_0_, bf16[128,3584]{1,0:T(8,128)(2,1)S(1)} %get-tuple-element.37.normed, f32[7,128]{1,0:T(8,128)S(1)} %get-tuple-element.38.bias_query, f32[128,128]{1,0:T(8,128)S(1)} %get-tuple-element.35.refs_8_.cosine, ...), custom_call_target="tpu_custom_call" | custom-call | flops 822083584 | bytes 7000000 | tf_op jit(solution)/shard_map/pallas_call | solution.py:267
  36.2 1.3 %shard_map.123 = (f32[896,128]{1,0:T(8,128)S(1)}, f32[896,128]{1,0:T(8,128)S(1)}, f32[896,128]{1,0:T(8,128)S(1)}) custom-call(s32[1]{0:T(128)} %bitcast.rank_ref.refs_0_, bf16[896,128]{1,0:T(8,128)(2,1)S(1)} %shard_map.121.refs_1_, f32[8,128]{1,0:T(8,128)S(1)} %get-tuple-element.43.refs_2_, f32[128,1]{1,0:T(8,128)S(1)} %get-tuple-element.44.refs_3_, ...), custom_call_target="tpu_custom_call" | custom-call | flops 469762048 | bytes 7340032 | tf_op jit(solution)/shard_map/pallas_call | solution.py:267
  37.5 0.0 collective-permute-done.11.refs_15_
  37.5 1.5 %collective-permute-start.13 = (bf16[2,128,128]{2,1,0:T(8,128)(2,1)S(1)}, bf16[2,128,128]{2,1,0:T(8,128)(2,1)S(1)}, u32[]{:S(2)}, u32[]{:S(2)}) collective-permute-start(bf16[2,128,128]{2,1,0:T(8,128)(2,1)S(1)} %collective-permute-done.11.refs_15_), channel_id=1, source_target_pairs={{0,4},{4,0},{8,12},{12,8},{16,20},{20,16},{24,28},{28,24},{1,5},{5... | collective-permute-start | bytes 196616 | tf_op jit(solution)/shard_map/ppermute | solution.py:18
  39.0 0.0 collective-permute-done.6.refs_9_
  39.0 0.8 %collective-permute-done.5.refs_8_ = bf16[2,256,128]{2,1,0:T(8,128)(2,1)S(1)} collective-permute-done((bf16[2,256,128]{2,1,0:T(8,128)(2,1)S(1)}, bf16[2,256,128]{2,1,0:T(8,128)(2,1)S(1)}, u32[]{:S(2)}, u32[]{:S(2)}) %collective-permute-start.5) | collective-permute-done | bytes 131104 | tf_op jit(solution)/shard_map/ppermute | solution.py:18
  39.8 0.0 collective-permute-done.8.refs_11_
  39.8 2.4 %shard_map.125 = (f32[896,128]{1,0:T(8,128)S(1)}, f32[896,128]{1,0:T(8,128)S(1)}, f32[896,128]{1,0:T(8,128)S(1)}) custom-call(s32[1]{0:T(128)} %bitcast.rank_ref.refs_0_, bf16[896,128]{1,0:T(8,128)(2,1)S(1)} %shard_map.121.refs_1_, f32[8,128]{1,0:T(8,128)S(1)} %get-tuple-element.43.refs_2_, f32[128,1]{1,0:T(8,128)S(1)} %get-tuple-element.44.refs_3_, ...), custom_call_target="tpu_custom_call" | custom-call | flops 763363328 | bytes 11927552 | tf_op jit(solution)/shard_map/pallas_call | solution.py:267
  42.2 0.0 collective-permute-done.12.refs_8_
  42.2 0.1 collective-permute-done.13.refs_9_
  42.2 1.5 %shard_map.127 = bf16[128,896]{1,0:T(8,128)(2,1)} custom-call(s32[1]{0:T(128)} %bitcast.rank_ref.refs_0_, bf16[896,128]{1,0:T(8,128)(2,1)S(1)} %shard_map.121.refs_1_, f32[8,128]{1,0:T(8,128)S(1)} %get-tuple-element.43.refs_2_, f32[128,1]{1,0:T(8,128)S(1)} %get-tuple-element.44.refs_3_, f32[128,1]{1,0:T(8,128)S(1)} %get-tuple-element.45.refs_4_, ...), custom_call_target="tpu_custom_call" | custom-call | flops 176160768 | bytes 2752512 | tf_op jit(solution)/shard_map/pallas_call | solution.py:267
  (3 shorter events, 0.1 us)
Async XLA Ops:
  0.0 8.8 %collective-permute-start = (bf16[128,896]{1,0:T(8,128)(2,1)}, bf16[128,896]{1,0:T(8,128)(2,1)S(1)}, u32[]{:S(2)}, u32[]{:S(2)}) collective-permute-start(bf16[128,896]{1,0:T(8,128)(2,1)} %refs_0_.1), channel_id=1, source_target_pairs={{0,2},{1,3},{2,0},{3,1},{4,6},{5,7},{6,4},{7,5},{8,10},{9,11},{10,... | collective-permute-start | bytes 688136 | tf_op jit(solution)/shard_map/ppermute | solution.py:18
  8.8 14.4 %collective-permute-start.1 = (bf16[256,896]{1,0:T(8,128)(2,1)S(1)}, bf16[256,896]{1,0:T(8,128)(2,1)S(1)}, u32[]{:S(2)}, u32[]{:S(2)}) collective-permute-start(bf16[256,896]{1,0:T(8,128)(2,1)S(1)} %shard_map.119.refs_1_), channel_id=1, source_target_pairs={{0,1},{1,0},{2,3},{3,2},{4,5},{5,4},{6,7},{7,6},{8,9},{9,8},{10,11... | collective-permute-start | bytes 1376264 | tf_op jit(solution)/shard_map/ppermute | solution.py:18
  9.8 9.8 %collective-permute-start.3 = (bf16[2,256,128]{2,1,0:T(8,128)(2,1)S(1)}, bf16[2,256,128]{2,1,0:T(8,128)(2,1)S(1)}, u32[]{:S(2)}, u32[]{:S(2)}) collective-permute-start(bf16[2,256,128]{2,1,0:T(8,128)(2,1)S(1)} %shard_map.122.refs_5_), channel_id=1, source_target_pairs={{0,16},{4,20},{8,24},{12,28},{16,0},{20,4},{24,8},{28,12},{1,17},{... | collective-permute-start | bytes 393224 | tf_op jit(solution)/shard_map/ppermute | solution.py:18
  19.7 6.6 %collective-permute-start.7 = (bf16[2,256,128]{2,1,0:T(8,128)(2,1)S(1)}, bf16[2,256,128]{2,1,0:T(8,128)(2,1)S(1)}, u32[]{:S(2)}, u32[]{:S(2)}) collective-permute-start(bf16[2,256,128]{2,1,0:T(8,128)(2,1)S(1)} %collective-permute-done.3.refs_7_), channel_id=1, source_target_pairs={{0,8},{4,12},{8,0},{12,4},{16,24},{20,28},{24,16},{28,20},{1,9},{5... | collective-permute-start | bytes 393224 | tf_op jit(solution)/shard_map/ppermute | solution.py:18
  20.4 8.5 %collective-permute-start.2 = (bf16[2,256,128]{2,1,0:T(8,128)(2,1)S(1)}, bf16[2,256,128]{2,1,0:T(8,128)(2,1)S(1)}, u32[]{:S(2)}, u32[]{:S(2)}) collective-permute-start(bf16[2,256,128]{2,1,0:T(8,128)(2,1)S(1)} %shard_map.122.refs_5_), channel_id=1, source_target_pairs={{0,8},{4,12},{8,0},{12,4},{16,24},{20,28},{24,16},{28,20},{1,9},{5... | collective-permute-start | bytes 393224 | tf_op jit(solution)/shard_map/ppermute | solution.py:18
  21.7 11.4 %collective-permute-start.4 = (bf16[2,256,128]{2,1,0:T(8,128)(2,1)S(1)}, bf16[2,256,128]{2,1,0:T(8,128)(2,1)S(1)}, u32[]{:S(2)}, u32[]{:S(2)}) collective-permute-start(bf16[2,256,128]{2,1,0:T(8,128)(2,1)S(1)} %shard_map.122.refs_5_), channel_id=1, source_target_pairs={{0,4},{4,0},{8,12},{12,8},{16,20},{20,16},{24,28},{28,24},{1,5},{5... | collective-permute-start | bytes 393224 | tf_op jit(solution)/shard_map/ppermute | solution.py:18
  24.2 6.8 %collective-permute-start.10 = (bf16[2,128,128]{2,1,0:T(8,128)(2,1)S(1)}, bf16[2,128,128]{2,1,0:T(8,128)(2,1)S(1)}, u32[]{:S(2)}, u32[]{:S(2)}) collective-permute-start(bf16[2,128,128]{2,1,0:T(8,128)(2,1)S(1)} %get-tuple-element.49.refs_0_.refs_12_), channel_id=1, source_target_pairs={{0,16},{4,20},{8,24},{12,28},{16,0},{20,4},{24,8},{28,12},{1,17},{... | collective-permute-start | bytes 196616 | tf_op jit(solution)/shard_map/ppermute | solution.py:18
  26.3 13.5 %collective-permute-start.8 = (bf16[2,384,128]{2,1,0:T(8,128)(2,1)S(1)}, bf16[2,384,128]{2,1,0:T(8,128)(2,1)S(1)}, u32[]{:S(2)}, u32[]{:S(2)}) collective-permute-start(bf16[2,384,128]{2,1,0:T(8,128)(2,1)S(1)} %shard_map.124), channel_id=1, source_target_pairs={{0,4},{4,0},{8,12},{12,8},{16,20},{20,16},{24,28},{28,24},{1,5},{5... | collective-permute-start | bytes 589832 | tf_op jit(solution)/shard_map/ppermute | solution.py:18
  28.4 4.3 %collective-permute-start.9 = (bf16[2,128,128]{2,1,0:T(8,128)(2,1)S(1)}, bf16[2,128,128]{2,1,0:T(8,128)(2,1)S(1)}, u32[]{:S(2)}, u32[]{:S(2)}) collective-permute-start(bf16[2,128,128]{2,1,0:T(8,128)(2,1)S(1)} %get-tuple-element.49.refs_0_.refs_12_), channel_id=1, source_target_pairs={{0,8},{4,12},{8,0},{12,4},{16,24},{20,28},{24,16},{28,20},{1,9},{5... | collective-permute-start | bytes 196616 | tf_op jit(solution)/shard_map/ppermute | solution.py:18
  28.9 10.1 %collective-permute-start.6 = (bf16[2,256,128]{2,1,0:T(8,128)(2,1)S(1)}, bf16[2,256,128]{2,1,0:T(8,128)(2,1)S(1)}, u32[]{:S(2)}, u32[]{:S(2)}) collective-permute-start(bf16[2,256,128]{2,1,0:T(8,128)(2,1)S(1)} %collective-permute-done.3.refs_7_), channel_id=1, source_target_pairs={{0,4},{4,0},{8,12},{12,8},{16,20},{20,16},{24,28},{28,24},{1,5},{5... | collective-permute-start | bytes 393224 | tf_op jit(solution)/shard_map/ppermute | solution.py:18
  30.9 8.8 %collective-permute-start.5 = (bf16[2,256,128]{2,1,0:T(8,128)(2,1)S(1)}, bf16[2,256,128]{2,1,0:T(8,128)(2,1)S(1)}, u32[]{:S(2)}, u32[]{:S(2)}) collective-permute-start(bf16[2,256,128]{2,1,0:T(8,128)(2,1)S(1)} %collective-permute-done.2.refs_6_), channel_id=1, source_target_pairs={{0,4},{4,0},{8,12},{12,8},{16,20},{20,16},{24,28},{28,24},{1,5},{5... | collective-permute-start | bytes 393224 | tf_op jit(solution)/shard_map/ppermute | solution.py:18
  32.6 9.5 %collective-permute-start.12 = (bf16[2,256,128]{2,1,0:T(8,128)(2,1)S(1)}, bf16[2,256,128]{2,1,0:T(8,128)(2,1)S(1)}, u32[]{:S(2)}, u32[]{:S(2)}) collective-permute-start(bf16[2,256,128]{2,1,0:T(8,128)(2,1)S(1)} %shard_map.126), channel_id=1, source_target_pairs={{0,4},{4,0},{8,12},{12,8},{16,20},{20,16},{24,28},{28,24},{1,5},{5... | collective-permute-start | bytes 393224 | tf_op jit(solution)/shard_map/ppermute | solution.py:18
  33.0 4.4 %collective-permute-start.11 = (bf16[2,128,128]{2,1,0:T(8,128)(2,1)S(1)}, bf16[2,128,128]{2,1,0:T(8,128)(2,1)S(1)}, u32[]{:S(2)}, u32[]{:S(2)}) collective-permute-start(bf16[2,128,128]{2,1,0:T(8,128)(2,1)S(1)} %collective-permute-done.10.refs_14_.refs_1_), channel_id=1, source_target_pairs={{0,8},{4,12},{8,0},{12,4},{16,24},{20,28},{24,16},{28,20},{1,9},{5... | collective-permute-start | bytes 196616 | tf_op jit(solution)/shard_map/ppermute | solution.py:18
  37.5 4.7 %collective-permute-start.13 = (bf16[2,128,128]{2,1,0:T(8,128)(2,1)S(1)}, bf16[2,128,128]{2,1,0:T(8,128)(2,1)S(1)}, u32[]{:S(2)}, u32[]{:S(2)}) collective-permute-start(bf16[2,128,128]{2,1,0:T(8,128)(2,1)S(1)} %collective-permute-done.11.refs_15_), channel_id=1, source_target_pairs={{0,4},{4,0},{8,12},{12,8},{16,20},{20,16},{24,28},{28,24},{1,5},{5... | collective-permute-start | bytes 196616 | tf_op jit(solution)/shard_map/ppermute | solution.py:18
